TPU v7x, 128 devices: a whole 4x4x4 slice. The times are simulated.
128 devices in a mesh: req: 32 (over y, z, core), mp: 4 (over x).
Axes of the slice: x: 4, y: 4, z: 4, core: 2. Of those that a mesh axis runs over, the one named last changes fastest.
Arguments:
- hidden_in: bfloat16 [16384, 2048], P(('req', 'mp')), may hold values from -48 to 48
- segment_ids: int32 [32, 512], replicated, may hold values from 0 to 2, never falling along the last dimension, each value on 1 to 256 neighbouring positions
- request_prompt: int32 [1024], P('req'), may hold values from 0 to 95, as said below
- page_table: int32 [1024, 16], P('req'), may hold values from 0 to 511, as said below
- ln_attn: bfloat16 [2048], replicated, may hold values from 0.5 to 1.5
- w_query: bfloat16 [2048, 2048], P(None, 'mp'), may hold values from -0.125 to 0.125
- w_key: bfloat16 [2048, 1024], P(None, 'mp'), may hold values from -0.125 to 0.125
- w_value: bfloat16 [2048, 1024], P(None, 'mp'), may hold values from -0.125 to 0.125
- q_gain: bfloat16 [128], replicated, may hold values from 0.5 to 1.5
- k_gain: bfloat16 [128], replicated, may hold values from 0.5 to 1.5
- w_out: bfloat16 [2048, 2048], P('mp'), may hold values from -0.125 to 0.125
- ln_mlp: bfloat16 [2048], replicated, may hold values from 0.5 to 1.5
- w_gate: bfloat16 [2048, 3072], P(None, 'mp'), may hold values from -0.125 to 0.125
- w_up: bfloat16 [2048, 3072], P(None, 'mp'), may hold values from -0.125 to 0.125
- w_down: bfloat16 [3072, 2048], P('mp'), may hold values from -0.109375 to 0.109375
Outputs:
- layer_out: bfloat16 [16384, 2048], P(('req', 'mp'))
- kv_pages: bfloat16 [16384, 16, 8, 256], P('req', None, 'mp')
Inputs may be any that keep to these rules, and one draw needn't show every extreme that they name: `request_prompt`: every prompt is continued by 8 to 16 requests, and some prompt by exactly 16. `page_table`: the 32 rows of one index of req name each of the 512 pages once.
All inputs are finite; a program needn't handle non-finite values.
Results may differ from a plain program's by a relative error of at most 0.0075.
Values may be sent and summed in bfloat16 or wider, within the bound.
A program may use at most 128 MiB of HBM per device.

v0:
```python
import math

import jax
import jax.numpy as jnp
from jax import lax
from jax.sharding import PartitionSpec as P

HD = 128
PROMPTS_DEV = 3
PAGE = 16


EPS = 1e-06
THETA = 1000000.0


def rms_scale(values, gain):
    wide = values.astype(jnp.float32)
    return (
        wide
        * lax.rsqrt(jnp.mean(wide * wide, axis=-1, keepdims=True) + EPS)
        * gain.astype(jnp.float32)
    )


def segment_table(segment_row):
    member = (segment_row[:, None] == jnp.arange(PROMPTS_DEV, dtype=jnp.int32)[None, :]).astype(
        jnp.int32
    )
    lengths = jnp.sum(member, axis=0)
    starts = jnp.cumsum(lengths) - lengths
    index = jnp.arange(segment_row.shape[0], dtype=jnp.int32)
    position = index - jnp.sum(member * starts[None, :], axis=1)
    return (starts, lengths, position)


def rotate(values, position):
    half = HD // 2
    freq = THETA ** (-(jnp.arange(half, dtype=jnp.float32) * 2.0) / HD)
    angle = position.astype(jnp.float32)[:, None] * freq[None, :]
    cosine = jnp.cos(angle)[:, None, :]
    sine = jnp.sin(angle)[:, None, :]
    first = values[..., :half]
    second = values[..., half:]
    return jnp.concatenate(
        [first * cosine - second * sine, second * cosine + first * sine], axis=-1
    )


def body(
    hidden_in,
    segment_ids,
    request_prompt,
    page_table,
    ln_attn,
    w_query,
    w_key,
    w_value,
    q_gain,
    k_gain,
    w_out,
    ln_mlp,
    w_gate,
    w_up,
    w_down,
):
    parts = lax.axis_size("mp")
    owner_rows = hidden_in.shape[0]
    seq_rows = owner_rows * parts
    heads_here = w_query.shape[1] // HD
    kv_here = w_key.shape[1] // HD
    group = heads_here // kv_here
    group_index = lax.axis_index("req")
    segment_row = lax.dynamic_index_in_dim(segment_ids, group_index, 0, keepdims=False)
    unused_starts, unused_lengths, position = segment_table(segment_row)
    piece = lax.all_gather(hidden_in, "mp", axis=0, tiled=True)
    count = piece.shape[0]
    normed = rms_scale(piece, ln_attn).astype(jnp.bfloat16)
    query = jnp.dot(normed, w_query, preferred_element_type=jnp.float32).reshape(
        count, heads_here, HD
    )
    project_key = jnp.dot(normed, w_key, preferred_element_type=jnp.float32).reshape(
        count, kv_here, HD
    )
    project_value = jnp.dot(normed, w_value, preferred_element_type=jnp.float32).astype(
        jnp.bfloat16
    )
    query = (
        rotate(rms_scale(query, q_gain), position)
        .astype(jnp.bfloat16)
        .reshape(count, heads_here * HD)
    )
    project_key = (
        rotate(rms_scale(project_key, k_gain), position)
        .astype(jnp.bfloat16)
        .reshape(count, kv_here * HD)
    )
    joined = [query, project_key, project_value]
    projected = jnp.concatenate(joined, axis=1)
    query_width = heads_here * HD
    key_width = kv_here * HD
    query = projected[:, :query_width].reshape(seq_rows, kv_here, group, HD)
    key = projected[:, query_width : query_width + key_width].reshape(seq_rows, kv_here, HD)
    value = projected[:, query_width + key_width : query_width + 2 * key_width].reshape(
        seq_rows, kv_here, HD
    )
    block = min(512, seq_rows)
    blocks = seq_rows // block
    key_index = jnp.arange(seq_rows, dtype=jnp.int32)

    def attend_block(inputs):
        query_block, first = inputs
        scores = jnp.einsum(
            "qcgd,kcd->cgqk", query_block, key, preferred_element_type=jnp.float32
        ) / math.sqrt(HD)
        row_index = first + jnp.arange(block, dtype=jnp.int32)
        allowed = (segment_row[:, None] == segment_row[None, :]) & (
            key_index[None, :] <= row_index[:, None]
        )
        raised = jnp.where(allowed[None, None], jnp.exp(scores), 0.0)
        weights = (raised / jnp.sum(raised, axis=-1, keepdims=True)).astype(jnp.bfloat16)
        mixed = jnp.einsum("cgqk,kcd->qcgd", weights, value, preferred_element_type=jnp.float32)
        return mixed.astype(jnp.bfloat16).reshape(block, query_width)

    attended = lax.map(
        attend_block,
        (
            query.reshape(blocks, block, kv_here, group, HD),
            jnp.arange(blocks, dtype=jnp.int32) * block,
        ),
    )
    attended = attended.reshape(seq_rows, query_width)
    own_sum = lax.psum_scatter(
        jnp.dot(attended, w_out, preferred_element_type=jnp.float32).astype(jnp.bfloat16),
        "mp",
        scatter_dimension=0,
        tiled=True,
    ).astype(jnp.float32)
    after = (hidden_in.astype(jnp.float32) + own_sum).astype(jnp.bfloat16)
    normed_mlp = rms_scale(lax.all_gather(after, "mp", axis=0, tiled=True), ln_mlp).astype(
        jnp.bfloat16
    )
    gate = jnp.dot(normed_mlp, w_gate, preferred_element_type=jnp.float32)
    upper = jnp.dot(normed_mlp, w_up, preferred_element_type=jnp.float32)
    hidden = (jax.nn.silu(gate) * upper).astype(jnp.bfloat16)
    result = (
        after.astype(jnp.float32)
        + lax.psum_scatter(
            jnp.dot(hidden, w_down, preferred_element_type=jnp.float32).astype(jnp.bfloat16),
            "mp",
            scatter_dimension=0,
            tiled=True,
        ).astype(jnp.float32)
    ).astype(jnp.bfloat16)
    pairs = jnp.concatenate([key, value], axis=-1)
    all_starts, all_lengths, unused = jax.vmap(segment_table)(segment_ids)
    prompts = segment_ids.shape[0] * PROMPTS_DEV
    catalog = jnp.arange(prompts, dtype=jnp.int32)
    most_pages = page_table.shape[1]
    pool_pages = page_table.shape[0] * most_pages
    owner = (
        jnp.zeros((pool_pages,), jnp.int32)
        .at[page_table.reshape(-1)]
        .set(jnp.arange(pool_pages, dtype=jnp.int32))
    )
    request = owner // most_pages
    page = owner % most_pages
    picks = (request_prompt[:, None] == catalog[None, :]).astype(jnp.int32)
    request_begin = request_prompt // PROMPTS_DEV * seq_rows + jnp.sum(
        picks * all_starts.reshape(-1)[None, :], axis=1
    )
    request_length = jnp.sum(picks * all_lengths.reshape(-1)[None, :], axis=1)
    begin = request_begin[request]
    length = request_length[request]
    offset = page[:, None] * PAGE + jnp.arange(PAGE, dtype=jnp.int32)[None, :]
    valid = offset < length[:, None]
    source = jnp.where(valid, begin[:, None] + offset, 0)
    everything = lax.all_gather(pairs, "req", axis=0, tiled=True)
    taken = everything[source]
    cache = jnp.where(valid[:, :, None, None], taken, jnp.zeros((), jnp.bfloat16))
    return (result, cache)


def solution(mesh):
    return jax.shard_map(
        body,
        mesh=mesh,
        in_specs=(
            P(("req", "mp"), None),
            P(),
            P("req"),
            P("req", None),
            P(),
            P(None, "mp"),
            P(None, "mp"),
            P(None, "mp"),
            P(),
            P(),
            P("mp", None),
            P(),
            P(None, "mp"),
            P(None, "mp"),
            P("mp", None),
        ),
        out_specs=(P(("req", "mp"), None), P("req", None, "mp", None)),
        check_vma=False,
    )
```

profile of v0, /device:TPU:0, one launch (start us, length us, event | category | flops | bytes accessed | tf_op | source)
XLA Modules:
  0.0 345.3 jit_solution(5469853064702568555)
XLA Ops:
  8.0 0.8 convert_element_type.85
  11.8 0.8 copy.60
  13.5 0.9 fusion.9
  14.4 28.6 %all-gather.4.cloned.1.call-done = bf16[512,2048]{1,0:T(8,128)(2,1)} async-done(((bf16[128,2048]{1,0:T(8,128)(2,1)}), bf16[512,2048]{1,0:T(8,128)(2,1)}) %all-gather.4.cloned.1.call-update) | async-done | bytes 2097168 | tf_op jit(solution)/shard_map/all_gather | solution.py:76
  43.0 2.1 fusion
  45.1 3.6 %multiply_reduce_fusion = (f32[512,4]{0,1:T(4,128)S(1)}, f32[512,512]{0,1:T(8,128)S(1)}) fusion(bf16[2048,512]{1,0:T(8,128)(2,1)} %param.20, bf16[512,2048]{1,0:T(8,128)(2,1)} %all-gather.4.cloned.1.call-done, f32[2048]{0:T(1024)S(1)} %convert_element_type.85, f32[512]{0:T(512)S(1)} %add_rsqrt_fusion.3), kind=kOutput, calls=%fused_computation.25 | convolution fusion | flops 1078458368 | bytes 5261312 | tf_op jit(solution)/shard_map/dot_general | solution.py:79
  48.9 1.0 subtract_convert_fusion
  49.9 2.0 copy.62
  51.8 2.0 copy.61
  53.8 3.6 %multiply_reduce_fusion.1 = (f32[512,2]{0,1:T(2,128)S(1)}, f32[512,256]{0,1:T(8,128)}) fusion(bf16[2048,256]{1,0:T(8,128)(2,1)} %param.21, bf16[512,2048]{1,0:T(8,128)(2,1)} %all-gather.4.cloned.1.call-done, f32[2048]{0:T(1024)S(1)} %convert_element_type.85, f32[512]{0:T(512)S(1)} %add_rsqrt_fusion.3), kind=kOutput, calls=%fused_computation.40 | convolution fusion | flops 541326336 | bytes 3684352 | tf_op jit(solution)/shard_map/dot_general | solution.py:82
  57.4 2.0 copy.58
  59.4 1.3 multiply_multiply_fusion.1
  60.8 1.3 subtract_convert_fusion.1
  62.7 2.7 fusion.6
  65.4 1.0 convolution_convert_fusion.2
  66.4 1.3 fusion.8
  68.1 2.6 convolution_convert_fusion.1
  70.8 29.8 %reduce-scatter.3.cloned.1.call-done = bf16[128,2048]{1,0:T(8,128)(2,1)} async-done(((bf16[512,2048]{1,0:T(8,128)(2,1)}), bf16[128,2048]{1,0:T(8,128)(2,1)}) %reduce-scatter.3.cloned.1.call-update) | async-done | bytes 524304 | tf_op jit(solution)/shard_map/reduce_scatter | solution.py:133
  100.6 2.1 add_convert_fusion.1
  103.0 30.5 %all-gather.6.cloned.1.call-done = bf16[512,2048]{1,0:T(8,128)(2,1)} async-done(((bf16[128,2048]{1,0:T(8,128)(2,1)}), bf16[512,2048]{1,0:T(8,128)(2,1)}) %all-gather.6.cloned.1.call-update) | async-done | bytes 2097168 | tf_op jit(solution)/shard_map/all_gather | solution.py:140
  133.5 2.1 fusion.3
  135.6 5.5 %fusion.12 = f32[512,768]{1,0:T(8,128)} fusion(bf16[2048,768]{1,0:T(8,128)(2,1)} %param.27, bf16[512,2048]{1,0:T(8,128)(2,1)} %all-gather.6.cloned.1.call-done, f32[2048]{0:T(1024)S(1)} %convert_element_type.100, f32[512]{0:T(512)S(1)} %add_rsqrt_fusion.2), kind=kOutput, calls=%fused_computation.29 | convolution fusion | flops 1614807040 | bytes 6825984 | tf_op jit(solution)/shard_map/dot_general | solution.py:143
  141.1 8.3 %convolution_convert_fusion = bf16[512,2048]{1,0:T(8,128)(2,1)} fusion(bf16[768,2048]{1,0:T(8,128)(2,1)S(1)} %copy-done, f32[512,768]{1,0:T(8,128)} %fusion.12, bf16[2048,768]{1,0:T(8,128)(2,1)} %param.28, bf16[512,2048]{1,0:T(8,128)(2,1)} %all-gather.6.cloned.1.call-done, f32[2048]{0:T(1024)S(1)} %convert_element_type.100, f32[512]{0:T(512)S(1)} %add_rsqrt_fusion.2), kind=kOutput, calls=%fused_computation.16 | convolution fusion | flops 3228827648 | bytes 12068864 | tf_op jit(solution)/shard_map/dot_general | solution.py:149
  149.5 1.3 copy.67
  151.3 2.0 pad_maximum_fusion
  154.0 2.4 scatter_custom_fusion
  159.6 20.1 %select_select_fusion.1 = (s32[512]{0:T(512)S(1)}, pred[512]{0:T(512)(128)(4,1)S(1)}, pred[512]{0:T(512)(128)(4,1)S(1)}, pred[512]{0:T(512)(128)(4,1)S(1)}, pred...) fusion(s32[]{:T(128)} %bitcast.16, s32[]{:T(128)} %bitcast.17, ...), kind=kLoop, calls=%fused_computation.69 | loop fusion | flops 31744 | bytes 20096 | tf_op jit(solution)/shard_map/gather | solution.py:174
  179.7 20.0 %select_select_fusion = s32[512]{0:T(512)S(1)} fusion(pred[512]{0:T(512)(128)(4,1)S(1)} %get-tuple-element.56, pred[512]{0:T(512)(128)(4,1)S(1)} %get-tuple-element.55, pred[512]{0:T(512)(128)(4,1)S(1)} %get-tuple-element.54, pred[512]{0:T(512)(128)(4,1)S(1)} %get-tuple-element.53, pred[512]{0:T(512)(128)(4,1)S(1)} %get-tuple-element.52, ...), kind=kLoop, calls=%fused_computation.68 | loop fusion | flops 15872 | bytes 18048 | tf_op jit(solution)/shard_map/gather | solution.py:173
  200.4 2.0 add_convert_fusion
  202.3 51.4 %all-gather.8.cloned.1.call-done = bf16[16384,2,256]{2,1,0:T(2,128)(2,1)} async-done(((bf16[512,2,256]{2,1,0:T(2,128)(2,1)}), bf16[16384,2,256]{2,1,0:T(2,128)(2,1)}) %all-gather.8.cloned.1.call-update) | async-done | bytes 16777232 | tf_op jit(solution)/shard_map/all_gather | solution.py:178
  253.8 70.3 %gather_fusion = bf16[8192,2,256]{2,1,0:T(2,128)(2,1)} fusion(bf16[16384,2,256]{2,1,0:T(2,128)(2,1)} %all-gather.8.cloned.1.call-done, s32[8192]{0:T(1024)S(1)} %broadcast_clamp_fusion), kind=kCustom, calls=%fused_computation | custom fusion | bytes 16809984 | tf_op jit(solution)/shard_map/gather | solution.py:179
  324.1 14.7 %broadcast_select_fusion = bf16[512,16,2,256]{3,2,1,0:T(2,128)(2,1)} fusion(bf16[512,16,2,256]{3,2,1,0:T(2,128)(2,1)} %bitcast.112, pred[512,16]{1,0:T(8,128)(4,1)S(1)} %add_compare_fusion), kind=kLoop, calls=%fused_computation.2 | loop fusion | flops 4194304 | bytes 16785408 | tf_op jit(solution)/shard_map/jit(_where)/select_n | solution.py:180
  (84 shorter events, 11.1 us)
Async XLA Ops:
  7.2 133.9 %copy-start = (bf16[768,2048]{1,0:T(8,128)(2,1)S(1)}, bf16[768,2048]{1,0:T(8,128)(2,1)}, u32[]{:S(2)}) copy-start(bf16[768,2048]{1,0:T(8,128)(2,1)} %param.29) | copy-start | bytes 9437188
  7.2 35.8 %all-gather.4.cloned.1.call-start = ((), (), s32[]{:S(2)}) async-start(), calls=%async_computation.2 | async-start | bytes 2621440 | tf_op jit(solution)/shard_map/all_gather | solution.py:76
  7.9 92.6 %reduce-scatter.3.cloned.1.call-start = ((), (), s32[]{:S(2)}) async-start(), calls=%async_computation.3 | async-start | bytes 2621440 | tf_op jit(solution)/shard_map/reduce_scatter | solution.py:133
  59.4 3.3 copy-start.5
  59.4 3.3 copy-start.6
  62.0 0.7 copy-start.4
  62.7 2.7 copy-start.3
  62.7 2.7 copy-start.15
  65.4 1.0 copy-start.9
  66.4 1.4 copy-start.7
  66.4 1.7 copy-start.14
  70.7 32.2 %copy-start.12 = (bf16[2048]{0:T(1024)(128)(2,1)S(1)}, bf16[2048]{0:T(1024)(128)(2,1)}, u32[]{:S(2)}) copy-start(bf16[2048]{0:T(1024)(128)(2,1)} %param.26) | copy-start | bytes 12292
  70.7 62.8 %all-gather.6.cloned.1.call-start = ((), (), s32[]{:S(2)}) async-start(), calls=%async_computation.4 | async-start | bytes 2621440 | tf_op jit(solution)/shard_map/all_gather | solution.py:140
  102.7 97.7 %reduce-scatter.5.cloned.1.call-start = ((), (), s32[]{:S(2)}) async-start(), calls=%async_computation.5 | async-start | bytes 2621440 | tf_op jit(solution)/shard_map/reduce_scatter | solution.py:148
  149.4 1.7 copy-start.8
  149.4 3.9 %copy-start.10 = (s32[32,512]{1,0:T(8,128)S(1)}, s32[32,512]{1,0:T(8,128)}, u32[]{:S(2)}) copy-start(s32[32,512]{1,0:T(8,128)} %param.16) | copy-start | bytes 196612
  149.4 4.5 %copy-start.11 = (s32[32,16]{0,1:T(8,128)S(1)}, s32[32,16]{0,1:T(8,128)}, u32[]{:S(2)}) copy-start(s32[32,16]{0,1:T(8,128)} %param.18) | copy-start | bytes 6148
  149.4 7.1 %copy-start.13 = (s32[32]{0:T(128)S(1)}, s32[32]{0:T(128)}, u32[]{:S(2)}) copy-start(s32[32]{0:T(128)} %param.17) | copy-start | bytes 388
  149.4 51.0 %copy-start.2 = (bf16[128,2048]{1,0:T(8,128)(2,1)S(1)}, bf16[128,2048]{1,0:T(8,128)(2,1)}, u32[]{:S(2)}) copy-start(bf16[128,2048]{1,0:T(8,128)(2,1)} %add_convert_fusion.1) | copy-start | bytes 1572868
  149.4 104.3 %all-gather.8.cloned.1.call-start = ((), (), s32[]{:S(2)}) async-start(), calls=%async_computation.6 | async-start | bytes 17301504 | tf_op jit(solution)/shard_map/all_gather | solution.py:178
  324.1 14.7 %copy-start.1 = (bf16[768,2048]{1,0:T(8,128)(2,1)S(1)}, bf16[768,2048]{1,0:T(8,128)(2,1)}, u32[]{:S(2)}) copy-start(bf16[768,2048]{1,0:T(8,128)(2,1)} %param.29) | copy-start | bytes 9437188
Sparse Core Ops, SparseCore 0:
  9.7 33.2 all-gather.3
  70.8 29.6 reduce-scatter.2
  102.9 30.5 all-gather.5
  149.6 29.6 reduce-scatter.4
  181.4 72.3 all-gather.7
where the time goes:
time: 348 us; the launch traced here: 345 us
  waiting for transfers between devices  141 us (41%)
  local copies, waits for them, and re-layouts  87.4 us (25%)
  other arithmetic  73.7 us (21%)
  matrix products  28.6 us (8%)
  between operations  14.1 us (4%)
    gather x1, local copies, waits for them, and re-layouts, body(): taken = everything[source]  70.3 us
    all_gather x1, waiting for transfers between devices, body(): everything = lax.all_gather(pairs, 'req', axis=0, tiled=True)  51.4 us
    all_gather x1, waiting for transfers between devices, body(): lax.all_gather(after, 'mp', axis=0, tiled=True)  30.5 us
    reduce_scatter x1, waiting for transfers between devices, body(): lax.psum_scatter(jnp.dot(attended, w_out, preferred_element_type=jnp.floa...  29.8 us
    all_gather x1, waiting for transfers between devices, body(): piece = lax.all_gather(hidden_in, 'mp', axis=0, tiled=True)  28.6 us
    gather x1, other arithmetic, body(): length = request_length[request]  20.1 us
    gather x1, other arithmetic, body(): begin = request_begin[request]  20 us
    select_n x1, other arithmetic, body(): jnp.where(valid[:, :, None, None], taken, jnp.zeros((), jnp.bfloat16))  14.7 us
  transfers between devices with their start and end apart: 5, of which 4 were waited for; matrix products, arithmetic and copies ran while one was open for 17% of the time, Pallas kernels for 0%

commit v1 on v0

--- a/solution.py
+++ b/solution.py
@@ -3,6 +3,8 @@
 import jax
 import jax.numpy as jnp
 from jax import lax
+from jax.experimental import pallas as pl
+from jax.experimental.pallas import tpu as pltpu
 from jax.sharding import PartitionSpec as P
 
 HD = 128
@@ -45,6 +47,104 @@
     return jnp.concatenate(
         [first * cosine - second * sine, second * cosine + first * sine], axis=-1
     )
+
+
+def request_rows(segment_ids, request_prompt, seq_rows):
+    bound = jnp.arange(PROMPTS_DEV + 1, dtype=jnp.int32)
+    below = jnp.sum((segment_ids[:, None, :] < bound[None, :, None]).astype(jnp.int32), axis=2)
+    groups = segment_ids.shape[0]
+    first = below[:, :PROMPTS_DEV] + jnp.arange(groups, dtype=jnp.int32)[:, None] * seq_rows
+    counts = below[:, 1:] - below[:, :-1]
+    picks = request_prompt[:, None] == jnp.arange(groups * PROMPTS_DEV, dtype=jnp.int32)[None, :]
+    begin = jnp.sum(jnp.where(picks, first.reshape(-1)[None, :], 0), axis=1)
+    length = jnp.sum(jnp.where(picks, counts.reshape(-1)[None, :], 0), axis=1)
+    return begin, length
+
+
+SLOTS = 8
+
+
+def fill_kernel(begin_ref, length_ref, table_ref, rows_ref, out_ref, slots, zeros, in_sem, out_sem):
+    requests, most = table_ref.shape
+    span = most * PAGE
+    last = rows_ref.shape[0] - span
+    zeros[...] = jnp.zeros_like(zeros)
+
+    def fetch(r, slot):
+        at = jnp.minimum(begin_ref[r], last)
+        return pltpu.make_async_copy(
+            rows_ref.at[pl.ds(at, span)], slots.at[slot, pl.ds(0, span)], in_sem.at[slot]
+        )
+
+    def drain(slot):
+        pltpu.make_async_copy(
+            out_ref.at[pl.ds(0, most)], out_ref.at[pl.ds(0, most)], out_sem.at[slot]
+        ).wait()
+
+    ahead = SLOTS // 2
+    for r in range(ahead):
+        fetch(r, r).start()
+
+    @pl.loop(0, requests)
+    def _(r):
+        slot = lax.rem(r, SLOTS)
+        fetch(r, slot).wait()
+        begin, length = begin_ref[r], length_ref[r]
+        shift = begin - jnp.minimum(begin, last)
+        full = length // PAGE
+        rest = length - full * PAGE
+
+        @pl.when(rest > 0)
+        def _():
+            at = shift + full * PAGE
+            tail = slots[slot, pl.ds(at, PAGE)]
+            row = lax.broadcasted_iota(jnp.int32, tail.shape, 0)
+            slots[slot, pl.ds(at, PAGE)] = jnp.where(row < rest, tail, jnp.zeros_like(tail))
+
+        for e in range(most):
+            page = table_ref[r, e]
+
+            @pl.when(e * PAGE < length)
+            def _():
+                pltpu.make_async_copy(
+                    slots.at[slot, pl.ds(shift + e * PAGE, PAGE)], out_ref.at[page], out_sem.at[slot]
+                ).start()
+
+            @pl.when(e * PAGE >= length)
+            def _():
+                pltpu.make_async_copy(zeros, out_ref.at[page], out_sem.at[slot]).start()
+
+        @pl.when(r + ahead < requests)
+        def _():
+            other = lax.rem(r + ahead, SLOTS)
+
+            @pl.when(r + ahead >= SLOTS)
+            def _():
+                drain(other)
+
+            fetch(r + ahead, other).start()
+
+    for r in range(max(0, requests - SLOTS), requests):
+        drain(r % SLOTS)
+
+
+def fill_pages(begin, length, page_table, rows):
+    requests, most = page_table.shape
+    unit = rows.shape[1:]
+    smem = pl.BlockSpec(memory_space=pltpu.SMEM)
+    return pl.pallas_call(
+        fill_kernel,
+        out_shape=jax.ShapeDtypeStruct((requests * most, PAGE) + unit, rows.dtype),
+        in_specs=[smem, smem, smem, pl.BlockSpec(memory_space=pl.ANY)],
+        out_specs=pl.BlockSpec(memory_space=pl.ANY),
+        scratch_shapes=[
+            pltpu.VMEM((SLOTS, (most + 1) * PAGE) + unit, rows.dtype),
+            pltpu.VMEM((PAGE,) + unit, rows.dtype),
+            pltpu.SemaphoreType.DMA((SLOTS,)),
+            pltpu.SemaphoreType.DMA((SLOTS,)),
+        ],
+        name="fill_pages",
+    )(begin, length, page_table, rows)
 
 
 def body(
@@ -153,31 +253,9 @@
         ).astype(jnp.float32)
     ).astype(jnp.bfloat16)
     pairs = jnp.concatenate([key, value], axis=-1)
-    all_starts, all_lengths, unused = jax.vmap(segment_table)(segment_ids)
-    prompts = segment_ids.shape[0] * PROMPTS_DEV
-    catalog = jnp.arange(prompts, dtype=jnp.int32)
-    most_pages = page_table.shape[1]
-    pool_pages = page_table.shape[0] * most_pages
-    owner = (
-        jnp.zeros((pool_pages,), jnp.int32)
-        .at[page_table.reshape(-1)]
-        .set(jnp.arange(pool_pages, dtype=jnp.int32))
-    )
-    request = owner // most_pages
-    page = owner % most_pages
-    picks = (request_prompt[:, None] == catalog[None, :]).astype(jnp.int32)
-    request_begin = request_prompt // PROMPTS_DEV * seq_rows + jnp.sum(
-        picks * all_starts.reshape(-1)[None, :], axis=1
-    )
-    request_length = jnp.sum(picks * all_lengths.reshape(-1)[None, :], axis=1)
-    begin = request_begin[request]
-    length = request_length[request]
-    offset = page[:, None] * PAGE + jnp.arange(PAGE, dtype=jnp.int32)[None, :]
-    valid = offset < length[:, None]
-    source = jnp.where(valid, begin[:, None] + offset, 0)
+    begin, length = request_rows(segment_ids, request_prompt, seq_rows)
     everything = lax.all_gather(pairs, "req", axis=0, tiled=True)
-    taken = everything[source]
-    cache = jnp.where(valid[:, :, None, None], taken, jnp.zeros((), jnp.bfloat16))
+    cache = fill_pages(begin, length, page_table, everything)
     return (result, cache)
 
 

time: 348 us -> 274 us (0.79)
  local copies, waits for them, and re-layouts: 87.4 us -> 16 us
  other arithmetic: 73.7 us -> 20 us
  waiting for transfers between devices: 141 us -> 182 us
  Pallas kernels: 0 us -> 11.7 us
    gather x5 -> x0, local copies, waits for them, and re-layouts: 73.1 us -> none  [the longest x1 70.3 us: body(): taken = everything[source]]
    gather x3 -> x0, other arithmetic: 40.1 us -> none  [the longest x1 20.1 us: body(): length = request_length[request]]
    all_gather x1, waiting for transfers between devices: 51.4 us -> 72.4 us  [body(): everything = lax.all_gather(pairs, 'req', axis=0, tiled=True)]
    reduce_scatter x1, waiting for transfers between devices: 0.02 us -> 19.8 us  [body(): lax.psum_scatter(jnp.dot(hidden, w_down, preferred_element_type=jnp.float...]
    select_n x3 -> x0, other arithmetic: 15 us -> none  [the longest x1 14.7 us: body(): jnp.where(valid[:, :, None, None], taken, jnp.zeros((), jnp.bfloat16))]
    pallas_call x0 -> x1, Pallas kernels: none -> 11.7 us  [fill_pages(): pl.pallas_call(fill_kernel, out_shape=jax.ShapeDtypeStruct((requests * mo...]
    another operation x6 -> x4, local copies, waits for them, and re-layouts: 5.68 us -> 7.08 us
  transfers between devices with their start and end apart: 5 -> 5, of which waited for: 4 -> 5; matrix products, arithmetic and copies ran while one was open for 17% -> 7% of each run, Pallas kernels for 0% -> 0%
where the time goes in v1:
time: 274 us; the launch traced here: 271 us
  waiting for transfers between devices  182 us (66%)
  matrix products  27.5 us (10%)
  other arithmetic  20 us (7%)
  local copies, waits for them, and re-layouts  16 us (6%)
  between operations  14 us (5%)
  Pallas kernels  11.7 us (4%)
    all_gather x1, waiting for transfers between devices, body(): everything = lax.all_gather(pairs, 'req', axis=0, tiled=True)  72.4 us
    all_gather x1, waiting for transfers between devices, body(): lax.all_gather(after, 'mp', axis=0, tiled=True)  30.5 us
    reduce_scatter x1, waiting for transfers between devices, body(): lax.psum_scatter(jnp.dot(attended, w_out, preferred_element_type=jnp.floa...  29.8 us
    all_gather x1, waiting for transfers between devices, body(): piece = lax.all_gather(hidden_in, 'mp', axis=0, tiled=True)  28.6 us
    reduce_scatter x1, waiting for transfers between devices, body(): lax.psum_scatter(jnp.dot(hidden, w_down, preferred_element_type=jnp.float...  19.8 us
    pallas_call x1, Pallas kernels, fill_pages(): pl.pallas_call(fill_kernel, out_shape=jax.ShapeDtypeStruct((requests * mo...  11.7 us
    dot_general x1, matrix products, body(): jnp.dot(hidden, w_down, preferred_element_type=jnp.float32)  8.31 us
    another operation x4, local copies, waits for them, and re-layouts  7.08 us
  transfers between devices with their start and end apart: 5, of which 5 were waited for; matrix products, arithmetic and copies ran while one was open for 7% of the time, Pallas kernels for 0%

profile of v1, /device:TPU:0, one launch (start us, length us, event | category | flops | bytes accessed | tf_op | source)
XLA Modules:
  0.0 271.3 jit_solution(1247149869099625819)
XLA Ops:
  8.0 0.9 constant_dynamic-slice_fusion
  9.8 0.9 copy.60
  10.6 0.8 copy.61
  13.5 0.9 fusion.9
  14.4 28.6 %all-gather.4.cloned.1.call-done = bf16[512,2048]{1,0:T(8,128)(2,1)} async-done(((bf16[128,2048]{1,0:T(8,128)(2,1)}), bf16[512,2048]{1,0:T(8,128)(2,1)}) %all-gather.4.cloned.1.call-update) | async-done | bytes 2097168 | tf_op jit(solution)/shard_map/all_gather | solution.py:176
  43.0 2.1 fusion
  45.1 3.6 %multiply_reduce_fusion.1 = (f32[512,2]{0,1:T(2,128)S(1)}, f32[512,256]{0,1:T(8,128)}) fusion(bf16[2048,256]{1,0:T(8,128)(2,1)} %param.21, bf16[512,2048]{1,0:T(8,128)(2,1)} %all-gather.4.cloned.1.call-done, f32[2048]{0:T(1024)S(1)} %convert_element_type.84, f32[512]{0:T(512)S(1)} %add_rsqrt_fusion.3), kind=kOutput, calls=%fused_computation.36 | convolution fusion | flops 541326336 | bytes 3684352 | tf_op jit(solution)/shard_map/dot_general | solution.py:182
  48.7 2.0 copy.59
  50.7 3.6 %multiply_reduce_fusion = (f32[512,4]{0,1:T(4,128)S(1)}, f32[512,512]{0,1:T(8,128)S(1)}) fusion(bf16[2048,512]{1,0:T(8,128)(2,1)} %param.20, bf16[512,2048]{1,0:T(8,128)(2,1)} %all-gather.4.cloned.1.call-done, f32[2048]{0:T(1024)S(1)} %convert_element_type.84, f32[512]{0:T(512)S(1)} %add_rsqrt_fusion.3), kind=kOutput, calls=%fused_computation.22 | convolution fusion | flops 1078458368 | bytes 5261312 | tf_op jit(solution)/shard_map/dot_general | solution.py:179
  54.6 1.0 subtract_convert_fusion
  55.5 2.0 copy.62
  57.5 2.0 copy.63
  59.5 1.3 multiply_multiply_fusion.1
  60.8 1.3 subtract_convert_fusion.1
  62.9 1.6 fusion.6
  64.7 0.9 convolution_convert_fusion.2
  65.7 1.3 fusion.8
  67.4 2.6 convolution_convert_fusion.1
  70.1 29.8 %reduce-scatter.3.cloned.1.call-done = bf16[128,2048]{1,0:T(8,128)(2,1)} async-done(((bf16[512,2048]{1,0:T(8,128)(2,1)}), bf16[128,2048]{1,0:T(8,128)(2,1)}) %reduce-scatter.3.cloned.1.call-update) | async-done | bytes 524304 | tf_op jit(solution)/shard_map/reduce_scatter | solution.py:233
  99.9 2.1 add_convert_fusion.1
  102.3 30.5 %all-gather.6.cloned.1.call-done = bf16[512,2048]{1,0:T(8,128)(2,1)} async-done(((bf16[128,2048]{1,0:T(8,128)(2,1)}), bf16[512,2048]{1,0:T(8,128)(2,1)}) %all-gather.6.cloned.1.call-update) | async-done | bytes 2097168 | tf_op jit(solution)/shard_map/all_gather | solution.py:240
  132.8 2.1 fusion.3
  134.9 5.5 %fusion.12 = f32[512,768]{1,0:T(8,128)} fusion(bf16[2048,768]{1,0:T(8,128)(2,1)} %param.27, bf16[512,2048]{1,0:T(8,128)(2,1)} %all-gather.6.cloned.1.call-done, f32[2048]{0:T(1024)S(1)} %convert_element_type.99, f32[512]{0:T(512)S(1)} %add_rsqrt_fusion.2), kind=kOutput, calls=%fused_computation.25 | convolution fusion | flops 1614807040 | bytes 6825984 | tf_op jit(solution)/shard_map/dot_general | solution.py:243
  140.4 8.3 %convolution_convert_fusion = bf16[512,2048]{1,0:T(8,128)(2,1)} fusion(bf16[768,2048]{1,0:T(8,128)(2,1)S(1)} %copy-done, f32[512,768]{1,0:T(8,128)} %fusion.12, bf16[2048,768]{1,0:T(8,128)(2,1)} %param.28, bf16[512,2048]{1,0:T(8,128)(2,1)} %all-gather.6.cloned.1.call-done, f32[2048]{0:T(1024)S(1)} %convert_element_type.99, f32[512]{0:T(512)S(1)} %add_rsqrt_fusion.2), kind=kOutput, calls=%fused_computation.13 | convolution fusion | flops 3228827648 | bytes 12068864 | tf_op jit(solution)/shard_map/dot_general | solution.py:249
  148.8 1.2 copy.67
  150.0 1.9 copy.68
  151.9 1.8 copy.69
  153.7 3.0 %pad_maximum_fusion = bf16[512,2,256]{2,1,0:T(2,128)(2,1)} fusion(bf16[512,2,128]{2,1,0:T(2,128)(2,1)} %copy.69, bf16[512,2,64]{2,1,0:T(2,128)(2,1)} %copy.68, bf16[512,2,64]{2,1,0:T(2,128)(2,1)S(1)} %copy.67), kind=kLoop, calls=%fused_computation.30 | loop fusion | flops 1572864 | bytes 1048576 | tf_op jit(solution)/shard_map/concatenate | solution.py:255
  158.8 19.8 %reduce-scatter.5.cloned.1.call-done = bf16[128,2048]{1,0:T(8,128)(2,1)} async-done(((bf16[512,2048]{1,0:T(8,128)(2,1)}), bf16[128,2048]{1,0:T(8,128)(2,1)}) %reduce-scatter.5.cloned.1.call-update) | async-done | bytes 524304 | tf_op jit(solution)/shard_map/reduce_scatter | solution.py:248
  178.6 2.1 add_convert_fusion
  180.7 72.4 %all-gather.8.cloned.1.call-done.rows_ref = bf16[16384,2,256]{2,1,0:T(2,128)(2,1)} async-done(((bf16[512,2,256]{2,1,0:T(2,128)(2,1)}), bf16[16384,2,256]{2,1,0:T(2,128)(2,1)}) %all-gather.8.cloned.1.call-update) | async-done | bytes 16777232 | tf_op jit(solution)/shard_map/all_gather | solution.py:257
  253.1 11.7 %fill_pages.1 = bf16[512,16,2,256]{3,2,1,0:T(2,128)(2,1)} custom-call(s32[32]{0:T(128)} %get-tuple-element.17.begin_ref, s32[32]{0:T(128)} %get-tuple-element.16.length_ref, s32[32,16]{1,0:T(8,128)} %copy.70.table_ref, bf16[16384,2,256]{2,1,0:T(2,128)(2,1)} %all-gather.8.cloned.1.call-done.rows_ref), custom_call_target="tpu_custom_call" | custom-call | tf_op jit(solution)/shard_map/fill_pages/pallas_call | solution.py:135
  (63 shorter events, 7.8 us)
Async XLA Ops:
  7.2 133.2 %copy-start = (bf16[768,2048]{1,0:T(8,128)(2,1)S(1)}, bf16[768,2048]{1,0:T(8,128)(2,1)}, u32[]{:S(2)}) copy-start(bf16[768,2048]{1,0:T(8,128)(2,1)} %param.29) | copy-start | bytes 9437188
  7.2 35.8 %all-gather.4.cloned.1.call-start = ((), (), s32[]{:S(2)}) async-start(), calls=%async_computation.2 | async-start | bytes 2621440 | tf_op jit(solution)/shard_map/all_gather | solution.py:176
  7.9 92.0 %reduce-scatter.3.cloned.1.call-start = ((), (), s32[]{:S(2)}) async-start(), calls=%async_computation.3 | async-start | bytes 2621440 | tf_op jit(solution)/shard_map/reduce_scatter | solution.py:233
  55.5 7.4 %copy-start.7 = (pred[512,512]{0,1:T(8,128)(4,1)S(1)}, pred[512,512]{0,1:T(8,128)(4,1)}, u32[]{:S(2)}) copy-start(pred[512,512]{0,1:T(8,128)(4,1)} %fusion.9) | copy-start | bytes 786436
  59.5 3.4 %copy-start.4 = (bf16[512,4,64]{2,0,1:T(8,128)(2,1)S(1)}, bf16[512,4,64]{2,0,1:T(8,128)(2,1)}, u32[]{:S(2)}) copy-start(bf16[512,4,64]{2,0,1:T(8,128)(2,1)} %copy.62) | copy-start | bytes 786436
  59.5 3.4 %copy-start.5 = (bf16[512,4,64]{2,0,1:T(8,128)(2,1)S(1)}, bf16[512,4,64]{2,0,1:T(8,128)(2,1)}, u32[]{:S(2)}) copy-start(bf16[512,4,64]{2,0,1:T(8,128)(2,1)} %copy.63) | copy-start | bytes 786436
  62.1 0.7 copy-start.2
  62.1 0.8 copy-start.3
  62.9 1.6 copy-start.1
  62.9 1.9 copy-start.13
  65.7 1.3 copy-start.6
  65.7 1.7 copy-start.12
  70.0 32.2 %copy-start.10 = (bf16[2048]{0:T(1024)(128)(2,1)S(1)}, bf16[2048]{0:T(1024)(128)(2,1)}, u32[]{:S(2)}) copy-start(bf16[2048]{0:T(1024)(128)(2,1)} %param.26) | copy-start | bytes 12292
  70.0 62.8 %all-gather.6.cloned.1.call-start = ((), (), s32[]{:S(2)}) async-start(), calls=%async_computation.4 | async-start | bytes 2621440 | tf_op jit(solution)/shard_map/all_gather | solution.py:240
  102.0 76.5 %reduce-scatter.5.cloned.1.call-start = ((), (), s32[]{:S(2)}) async-start(), calls=%async_computation.5 | async-start | bytes 2621440 | tf_op jit(solution)/shard_map/reduce_scatter | solution.py:248
  148.7 8.1 %copy-start.8 = (s32[32,512]{1,0:T(8,128)S(1)}, s32[32,512]{1,0:T(8,128)}, u32[]{:S(2)}) copy-start(s32[32,512]{1,0:T(8,128)} %param.16) | copy-start | bytes 196612
  148.7 8.7 %copy-start.9 = (s32[32,16]{0,1:T(8,128)S(1)}, s32[32,16]{0,1:T(8,128)}, u32[]{:S(2)}) copy-start(s32[32,16]{0,1:T(8,128)} %param.18) | copy-start | bytes 6148
  148.7 9.3 %copy-start.11 = (s32[32]{0:T(128)S(1)}, s32[32]{0:T(128)}, u32[]{:S(2)}) copy-start(s32[32]{0:T(128)} %param.17) | copy-start | bytes 388
  148.7 104.3 %all-gather.8.cloned.1.call-start = ((), (), s32[]{:S(2)}) async-start(), calls=%async_computation.6 | async-start | bytes 17301504 | tf_op jit(solution)/shard_map/all_gather | solution.py:257
Sparse Core Ops, SparseCore 0:
  9.7 33.2 all-gather.3
  70.1 29.6 reduce-scatter.2
  102.2 30.5 all-gather.5
  148.9 29.6 reduce-scatter.4
  180.7 72.3 all-gather.7

commit v2 on v1

v2 whole, which is shorter than its diff:
```python
import math

import jax
import jax.numpy as jnp
from jax import lax
from jax.experimental import pallas as pl
from jax.experimental.pallas import tpu as pltpu
from jax.sharding import PartitionSpec as P

HD = 128
PROMPTS_DEV = 3
PAGE = 16


EPS = 1e-06
THETA = 1000000.0


def request_rows(segment_ids, request_prompt, seq_rows):
    bound = jnp.arange(PROMPTS_DEV + 1, dtype=jnp.int32)
    below = jnp.sum((segment_ids[:, None, :] < bound[None, :, None]).astype(jnp.int32), axis=2)
    groups = segment_ids.shape[0]
    first = below[:, :PROMPTS_DEV] + jnp.arange(groups, dtype=jnp.int32)[:, None] * seq_rows
    counts = below[:, 1:] - below[:, :-1]
    picks = request_prompt[:, None] == jnp.arange(groups * PROMPTS_DEV, dtype=jnp.int32)[None, :]
    begin = jnp.sum(jnp.where(picks, first.reshape(-1)[None, :], 0), axis=1)
    length = jnp.sum(jnp.where(picks, counts.reshape(-1)[None, :], 0), axis=1)
    return begin, length


SLOTS = 8


def fill_kernel(begin_ref, length_ref, table_ref, rows_ref, out_ref, slots, zeros, in_sem, out_sem):
    requests, most = table_ref.shape
    span = most * PAGE
    last = rows_ref.shape[0] - span
    zeros[...] = jnp.zeros_like(zeros)

    def fetch(r, slot):
        at = jnp.minimum(begin_ref[r], last)
        return pltpu.make_async_copy(
            rows_ref.at[pl.ds(at, span)], slots.at[slot, pl.ds(0, span)], in_sem.at[slot]
        )

    def drain(slot):
        pltpu.make_async_copy(
            out_ref.at[pl.ds(0, most)], out_ref.at[pl.ds(0, most)], out_sem.at[slot]
        ).wait()

    ahead = SLOTS // 2
    for r in range(ahead):
        fetch(r, r).start()

    @pl.loop(0, requests)
    def _(r):
        slot = lax.rem(r, SLOTS)
        fetch(r, slot).wait()
        begin, length = begin_ref[r], length_ref[r]
        shift = begin - jnp.minimum(begin, last)
        full = length // PAGE
        rest = length - full * PAGE

        @pl.when(rest > 0)
        def _():
            at = shift + full * PAGE
            tail = slots[slot, pl.ds(at, PAGE)]
            row = lax.broadcasted_iota(jnp.int32, tail.shape, 0)
            slots[slot, pl.ds(at, PAGE)] = jnp.where(row < rest, tail, jnp.zeros_like(tail))

        for e in range(most):
            page = table_ref[r, e]

            @pl.when(e * PAGE < length)
            def _():
                pltpu.make_async_copy(
                    slots.at[slot, pl.ds(shift + e * PAGE, PAGE)], out_ref.at[page], out_sem.at[slot]
                ).start()

            @pl.when(e * PAGE >= length)
            def _():
                pltpu.make_async_copy(zeros, out_ref.at[page], out_sem.at[slot]).start()

        @pl.when(r + ahead < requests)
        def _():
            other = lax.rem(r + ahead, SLOTS)

            @pl.when(r + ahead >= SLOTS)
            def _():
                drain(other)

            fetch(r + ahead, other).start()

    for r in range(max(0, requests - SLOTS), requests):
        drain(r % SLOTS)


def fill_pages(begin, length, page_table, rows):
    requests, most = page_table.shape
    unit = rows.shape[1:]
    smem = pl.BlockSpec(memory_space=pltpu.SMEM)
    return pl.pallas_call(
        fill_kernel,
        out_shape=jax.ShapeDtypeStruct((requests * most, PAGE) + unit, rows.dtype),
        in_specs=[smem, smem, smem, pl.BlockSpec(memory_space=pl.ANY)],
        out_specs=pl.BlockSpec(memory_space=pl.ANY),
        scratch_shapes=[
            pltpu.VMEM((SLOTS, (most + 1) * PAGE) + unit, rows.dtype),
            pltpu.VMEM((PAGE,) + unit, rows.dtype),
            pltpu.SemaphoreType.DMA((SLOTS,)),
            pltpu.SemaphoreType.DMA((SLOTS,)),
        ],
        name="fill_pages",
    )(begin, length, page_table, rows)


MESH = pl.DeviceIdType.MESH
HALF = 64
SUBS = 2
SIDE = 4
UNIT = 128
PUMPS = SIDE * SIDE


def rms(wide, gain):
    return wide * lax.rsqrt(jnp.mean(wide * wide, axis=-1, keepdims=True) + EPS) * gain


def layer_kernel(
    hidden,
    seg,
    ln_attn,
    w_query,
    w_key,
    w_value,
    q_gain,
    k_gain,
    w_out,
    ln_mlp,
    w_gate,
    w_up,
    w_down,
    out,
    kv,
    hbuf,
    abuf,
    wq,
    wk,
    wv,
    wo,
    wg,
    wu,
    wd,
    qbuf,
    kbuf,
    vbuf,
    kvbuf,
    attbuf,
    actbuf,
    ownbuf,
    send2f,
    send1,
    recv1,
    send2,
    recv2,
    local_sem,
    ag1_send,
    ag1_recv,
    rs1_send,
    rs1_recv,
    ag2_send,
    ag2_recv,
    rs2_send,
    rs2_recv,
    kv_send,
    kv1_recv,
    kv2_recv,
    kv_pair_recv,
):
    x = lax.axis_index("mp")
    c = lax.axis_index("req")
    core = lax.rem(c, 2)
    z = lax.rem(c // 2, SIDE)
    y = c // (2 * SIDE)
    width = hidden.shape[1]
    rows = hidden.shape[0]
    sub = HALF // SUBS

    def turn(value):
        return lax.rem(value + 2 * SIDE, SIDE)

    def req_of(yy, zz, cc):
        return (yy * SIDE + zz) * 2 + cc

    x_near = ((c, turn(x + 1)), (c, turn(x - 1)))
    pair = (req_of(y, z, 1 - core), x)
    y_near = ((req_of(turn(y + 1), z, core), x), (req_of(turn(y - 1), z, core), x))
    z_near = ((req_of(y, turn(z + 1), core), x), (req_of(y, turn(z - 1), core), x))

    moves = []
    weights = ((w_query, wq), (w_key, wk), (w_value, wv), (w_out, wo), (w_gate, wg), (w_up, wu), (w_down, wd))
    for d in range(2):
        for p in range(SUBS):
            moves.append(
                pltpu.make_async_copy(
                    hidden.at[pl.ds(d * HALF + p * sub, sub)], hbuf.at[x, d, p], local_sem.at[d * SUBS + p]
                )
            )
    for n, (src, dst) in enumerate(weights):
        moves.append(pltpu.make_async_copy(src, dst, local_sem.at[2 * SUBS + n]))
    for move in moves:
        move.start()

    barrier = pltpu.get_barrier_semaphore()
    for near in x_near + y_near + z_near + (pair,):
        pl.semaphore_signal(barrier, inc=1, device_id=near, device_id_type=MESH)
    pl.semaphore_wait(barrier, 7)

    def remote(src, dst, send, recv, near):
        return pltpu.make_async_remote_copy(
            src_ref=src, dst_ref=dst, send_sem=send, recv_sem=recv, device_id=near, device_id_type=MESH
        )

    def gather_step(buf, send, recv, j, d, p):
        block = buf.at[turn(x - j) if d == 0 else turn(x + j), d, p]
        return remote(block, block, send.at[j, d, p], recv.at[j, d, p], x_near[d])

    def gather_advance(buf, send, recv, j):
        for p in range(SUBS):
            for d in range(2):
                gather_step(buf, send, recv, j - 1, d, p).wait_recv()

                @pl.when(j < SIDE - 1)
                def _():
                    gather_step(buf, send, recv, j, d, p).start()

    def ring_rows(buf, j):
        a, b = turn(x - j), turn(x + j)
        upper = buf[a, 0].reshape(HALF, width)
        lower = buf[b, 1].reshape(HALF, width)
        return jnp.concatenate([upper, lower], axis=0).astype(jnp.float32)

    for p in range(SUBS):
        for d in range(2):
            own = hidden.at[pl.ds(d * HALF + p * sub, sub)]
            remote(own, hbuf.at[x, d, p], ag1_send.at[0, d, p], ag1_recv.at[0, d, p], x_near[d]).start()

    seg_row = seg[pl.ds(c, 1), :]
    first1 = jnp.sum((seg_row < 1).astype(jnp.int32), axis=1, keepdims=True)
    first2 = jnp.sum((seg_row < 2).astype(jnp.int32), axis=1, keepdims=True)

    def begin_of(token):
        return jnp.where(token >= first2, first2, jnp.where(token >= first1, first1, 0))

    lane = lax.broadcasted_iota(jnp.int32, (1, HD), 1)
    freq = jnp.exp2(lax.rem(lane, HD // 2).astype(jnp.float32) * (-2.0 * math.log2(THETA) / HD))
    sign = jnp.where(lane < HD // 2, -1.0, 1.0)
    gain_attn = ln_attn[...].astype(jnp.float32)
    gain_mlp = ln_mlp[...].astype(jnp.float32)
    gain_q = q_gain[...].astype(jnp.float32)
    gain_k = k_gain[...].astype(jnp.float32)
    heads = wq.shape[1] // HD
    kv_heads = wk.shape[1] // HD
    group = heads // kv_heads

    for move in moves[: 2 * SUBS + 3]:
        move.wait()

    @pl.loop(0, SIDE)
    def _(j):
        @pl.when(j > 0)
        def _():
            gather_advance(hbuf, ag1_send, ag1_recv, j)

        a, b = turn(x - j), turn(x + j)
        normed = rms(ring_rows(hbuf, j), gain_attn).astype(jnp.bfloat16)
        row = lax.broadcasted_iota(jnp.int32, (rows, 1), 0)
        token = jnp.where(row < HALF, a, b) * rows + row
        angle = (token - begin_of(token)).astype(jnp.float32) * freq
        cosine = jnp.cos(angle)
        sine = jnp.sin(angle) * sign

        def turned(values, gain):
            scaled = rms(values, gain)
            return (scaled * cosine + pltpu.roll(scaled, HD // 2, 1) * sine).astype(jnp.bfloat16)

        query = jnp.dot(normed, wq[...], preferred_element_type=jnp.float32)
        key = jnp.dot(normed, wk[...], preferred_element_type=jnp.float32)
        value = jnp.dot(normed, wv[...], preferred_element_type=jnp.float32).astype(jnp.bfloat16)
        for h in range(heads):
            part = turned(query[:, h * HD : (h + 1) * HD], gain_q)
            qbuf[a, 0, :, h * HD : (h + 1) * HD] = part[:HALF]
            qbuf[b, 1, :, h * HD : (h + 1) * HD] = part[HALF:]
        for h in range(kv_heads):
            part = turned(key[:, h * HD : (h + 1) * HD], gain_k)
            mine = value[:, h * HD : (h + 1) * HD]
            kbuf[a, 0, :, h * HD : (h + 1) * HD] = part[:HALF]
            kbuf[b, 1, :, h * HD : (h + 1) * HD] = part[HALF:]
            both = jnp.concatenate([part, mine], axis=1)
            kvbuf[pl.ds(a * rows, HALF), h, :] = both[:HALF]
            kvbuf[pl.ds(b * rows + HALF, HALF), h, :] = both[HALF:]
        vbuf[a, 0] = value[:HALF]
        vbuf[b, 1] = value[HALF:]

    seq = SIDE * rows
    kv_own = pltpu.make_async_copy(kvbuf, kv.at[pl.ds(c * seq, seq)], local_sem.at[2 * SUBS + len(weights)])
    kv_own.start()

    flows = ((0, 0), (0, 1), (1, 0), (1, 1))

    def pump(p):
        b, k = lax.rem(p, SIDE), p // SIDE
        for f, (axis, d) in enumerate(flows):
            sign_d = 1 if d == 0 else -1
            first = y_near[d] if axis == 0 else z_near[d]
            second = z_near[d] if axis == 0 else y_near[d]
            if axis == 0:
                oy, oz = turn(y - sign_d * b), turn(z - sign_d * k)
            else:
                oy, oz = turn(y - sign_d * k), turn(z - sign_d * b)
            at = req_of(oy, oz, core) * seq + f * UNIT
            block = kv.at[pl.ds(pl.multiple_of(at, UNIT), UNIT)]

            @pl.when((p >= 1) & (p < SIDE))
            def _():
                remote(block, block, kv_send.at[0], kv1_recv.at[f, p - 1], first).wait_recv()

            @pl.when(p >= SIDE)
            def _():
                remote(block, block, kv_send.at[0], kv2_recv.at[f, p - SIDE], second).wait_recv()

            @pl.when(p < SIDE - 1)
            def _():
                remote(block, block, kv_send.at[0], kv1_recv.at[f, p], first).start()

            @pl.when(p < PUMPS - SIDE)
            def _():
                remote(block, block, kv_send.at[0], kv2_recv.at[f, p], second).start()

            remote(block, block, kv_send.at[0], kv_pair_recv.at[0], pair).start()

    kv_own.wait()
    pump(jnp.int32(0))

    keys = kbuf[...].reshape(seq, kv_heads * HD)
    values = vbuf[...].reshape(seq, kv_heads * HD)
    for i in range(SIDE):
        extent = (i + 1) * rows
        token = lax.broadcasted_iota(jnp.int32, (rows, extent), 0) + i * rows
        other = lax.broadcasted_iota(jnp.int32, (rows, extent), 1)
        allowed = (other <= token) & (other >= begin_of(token[:, :1]))
        allowed = jnp.concatenate([allowed.astype(jnp.float32)] * group, axis=0) > 0.5
        block = qbuf[i].reshape(rows, heads * HD)
        for n in range(kv_heads):
            stacked = jnp.concatenate(
                [block[:, (n * group + h) * HD : (n * group + h + 1) * HD] for h in range(group)], axis=0
            )
            scores = lax.dot_general(
                stacked,
                keys[:extent, n * HD : (n + 1) * HD],
                (((1,), (1,)), ((), ())),
                preferred_element_type=jnp.float32,
            )
            raised = jnp.where(allowed, jnp.exp(scores * (1.0 / math.sqrt(HD))), 0.0)
            share = (raised * (1.0 / jnp.sum(raised, axis=-1, keepdims=True))).astype(jnp.bfloat16)
            mixed = jnp.dot(
                share, values[:extent, n * HD : (n + 1) * HD], preferred_element_type=jnp.float32
            ).astype(jnp.bfloat16)
            for h in range(group):
                at = (n * group + h) * HD
                attbuf[i, 0, :, at : at + HD] = mixed[h * rows : h * rows + HALF]
                attbuf[i, 1, :, at : at + HD] = mixed[h * rows + HALF : (h + 1) * rows]
    pump(jnp.int32(1))

    piece = width // SUBS

    def sum_step(send_buf, recv_buf, send, recv, j, d, n):
        return remote(send_buf.at[j, d, n], recv_buf.at[j, d, n], send.at[j, d, n], recv.at[j, d, n], x_near[d])

    def add_arrived(part, send_buf, recv_buf, send, recv, j, n):
        for d in range(2):
            sum_step(send_buf, recv_buf, send, recv, j, d, n).wait_recv()
        return part + jnp.concatenate([recv_buf[j, 0, n], recv_buf[j, 1, n]], axis=0).astype(jnp.float32)

    def send_on(part, send_buf, recv_buf, send, recv, j, n):
        rounded = part.astype(jnp.bfloat16)
        for d in range(2):
            send_buf[j, d, n] = rounded[d * HALF : (d + 1) * HALF]
            sum_step(send_buf, recv_buf, send, recv, j, d, n).start()

    ring1 = (send1, recv1, rs1_send, rs1_recv)
    ring2 = (send2, recv2, rs2_send, rs2_recv)

    moves[2 * SUBS + 3].wait()

    def out_rows(j):
        return jnp.concatenate([attbuf[turn(x - 1 - j), 0], attbuf[turn(x + 1 + j), 1]], axis=0)

    def out_part(mixed, n):
        return jnp.dot(mixed, wo[:, n * piece : (n + 1) * piece], preferred_element_type=jnp.float32)

    mixed = out_rows(0)
    for n in range(SUBS):
        send_on(out_part(mixed, n), *ring1, 0, n)

    @pl.loop(1, SIDE - 1)
    def _(j):
        mixed = out_rows(j)
        for n in range(SUBS):
            part = out_part(mixed, n)
            part = add_arrived(part, *ring1, j - 1, n)
            send_on(part, *ring1, j, n)
        pump(j + 1)

    mixed = out_rows(SIDE - 1)
    for n in range(SUBS):
        part = add_arrived(out_part(mixed, n), *ring1, SIDE - 2, n)
        for d in range(2):
            before = hbuf[x, d, :, :, n * piece : (n + 1) * piece].astype(jnp.float32)
            total = before + part[d * HALF : (d + 1) * HALF].reshape(SUBS, sub, piece)
            abuf[x, d, :, :, n * piece : (n + 1) * piece] = total.astype(jnp.bfloat16)
    for p in range(SUBS):
        for d in range(2):
            gather_step(abuf, ag2_send, ag2_recv, 0, d, p).start()
    pump(jnp.int32(SIDE))

    for move in moves[2 * SUBS + 4 :]:
        move.wait()

    def activation(j):
        normed = rms(ring_rows(abuf, j), gain_mlp).astype(jnp.bfloat16)
        gate = jnp.dot(normed, wg[...], preferred_element_type=jnp.float32)
        upper = jnp.dot(normed, wu[...], preferred_element_type=jnp.float32)
        return (gate * jax.nn.sigmoid(gate) * upper).astype(jnp.bfloat16)

    def down_part(act, n):
        return jnp.dot(act, wd[:, n * piece : (n + 1) * piece], preferred_element_type=jnp.float32)

    @pl.loop(0, SIDE)
    def _(j):
        @pl.when(j > 0)
        def _():
            gather_advance(abuf, ag2_send, ag2_recv, j)

        actbuf[...] = activation(j)
        pump(2 * j + SIDE + 1)

        @pl.when(j > 0)
        def _():
            act = actbuf[...]
            for n in range(SUBS):
                part = down_part(act, n)
                send2f[n] = part

                @pl.when(j > 1)
                def _():
                    send2f[n] = add_arrived(send2f[n], *ring2, j - 2, n)

                send_on(send2f[n], *ring2, j - 1, n)

        @pl.when(j == 0)
        def _():
            ownbuf[...] = actbuf[...]

        pump(2 * j + SIDE + 2)

    act = ownbuf[...]
    for p in range(3 * SIDE + 1, PUMPS):
        pump(jnp.int32(p))
    for n in range(SUBS):
        part = add_arrived(down_part(act, n), *ring2, SIDE - 2, n)
        for d in range(2):
            before = abuf[x, d, :, :, n * piece : (n + 1) * piece].reshape(HALF, piece).astype(jnp.float32)
            total = before + part[d * HALF : (d + 1) * HALF]
            out[d * HALF : (d + 1) * HALF, n * piece : (n + 1) * piece] = total.astype(jnp.bfloat16)

    @pl.loop(0, SIDE - 1)
    def _(j):
        for d in range(2):
            for p in range(SUBS):
                gather_step(hbuf, ag1_send, ag1_recv, j, d, p).wait_send()
                gather_step(abuf, ag2_send, ag2_recv, j, d, p).wait_send()
                sum_step(*ring1, j, d, p).wait_send()
                sum_step(*ring2, j, d, p).wait_send()

    sent = UNIT * len(flows) * (SIDE - 1 + PUMPS - SIDE + PUMPS)
    whole = kv.at[pl.ds(0, sent)]
    remote(whole, whole, kv_send.at[0], kv_pair_recv.at[0], pair).wait_send()
    got = kv.at[pl.ds(0, UNIT * len(flows) * PUMPS)]
    remote(got, got, kv_send.at[0], kv_pair_recv.at[0], pair).wait_recv()


def run_layer(hidden, seg, ln_attn, w_query, w_key, w_value, q_gain, k_gain, w_out, ln_mlp, w_gate, w_up, w_down):
    rows, width = hidden.shape
    seq = rows * SIDE
    units = w_gate.shape[1]
    kvw = w_key.shape[1]
    heads_w = w_query.shape[1]
    bf16, f32 = jnp.bfloat16, jnp.float32
    sub = HALF // SUBS
    vmem = pl.BlockSpec(memory_space=pltpu.VMEM)
    hbm = pl.BlockSpec(memory_space=pl.ANY)
    ring = (SIDE - 1, 2, SUBS)
    dma = pltpu.SemaphoreType.DMA
    blocks = pltpu.VMEM(ring + (HALF, width // SUBS), bf16)
    return pl.pallas_call(
        layer_kernel,
        out_shape=(
            jax.ShapeDtypeStruct((rows, width), bf16),
            jax.ShapeDtypeStruct((seg.shape[0] * seq, kvw // HD, 2 * HD), bf16),
        ),
        in_specs=[hbm, vmem, vmem, hbm, hbm, hbm, vmem, vmem, hbm, vmem, hbm, hbm, hbm],
        out_specs=(vmem, hbm),
        scratch_shapes=[
            pltpu.VMEM((SIDE, 2, SUBS, sub, width), bf16),
            pltpu.VMEM((SIDE, 2, SUBS, sub, width), bf16),
            pltpu.VMEM(w_query.shape, bf16),
            pltpu.VMEM(w_key.shape, bf16),
            pltpu.VMEM(w_value.shape, bf16),
            pltpu.VMEM(w_out.shape, bf16),
            pltpu.VMEM(w_gate.shape, bf16),
            pltpu.VMEM(w_up.shape, bf16),
            pltpu.VMEM(w_down.shape, bf16),
            pltpu.VMEM((SIDE, 2, HALF, heads_w), bf16),
            pltpu.VMEM((SIDE, 2, HALF, kvw), bf16),
            pltpu.VMEM((SIDE, 2, HALF, kvw), bf16),
            pltpu.VMEM((seq, kvw // HD, 2 * HD), bf16),
            pltpu.VMEM((SIDE, 2, HALF, heads_w), bf16),
            pltpu.VMEM((rows, units), bf16),
            pltpu.VMEM((rows, units), bf16),
            pltpu.VMEM((SUBS, rows, width // SUBS), f32),
            blocks,
            blocks,
            blocks,
            blocks,
            dma((2 * SUBS + 8,)),
        ]
        + [dma(ring)] * 8
        + [dma((1,)), dma((4, SIDE - 1)), dma((4, PUMPS - SIDE)), dma((1,))],
        compiler_params=pltpu.CompilerParams(
            collective_id=0, has_side_effects=True, vmem_limit_bytes=60 * 1024 * 1024
        ),
        name="layer",
    )(hidden, seg, ln_attn, w_query, w_key, w_value, q_gain, k_gain, w_out, ln_mlp, w_gate, w_up, w_down)


def body(
    hidden_in,
    segment_ids,
    request_prompt,
    page_table,
    ln_attn,
    w_query,
    w_key,
    w_value,
    q_gain,
    k_gain,
    w_out,
    ln_mlp,
    w_gate,
    w_up,
    w_down,
):
    begin, length = request_rows(segment_ids, request_prompt, segment_ids.shape[1])
    result, everything = run_layer(
        hidden_in,
        segment_ids,
        ln_attn[None, :],
        w_query,
        w_key,
        w_value,
        q_gain[None, :],
        k_gain[None, :],
        w_out,
        ln_mlp[None, :],
        w_gate,
        w_up,
        w_down,
    )
    return (result, fill_pages(begin, length, page_table, everything))


def solution(mesh):
    return jax.shard_map(
        body,
        mesh=mesh,
        in_specs=(
            P(("req", "mp"), None),
            P(),
            P("req"),
            P("req", None),
            P(),
            P(None, "mp"),
            P(None, "mp"),
            P(None, "mp"),
            P(),
            P(),
            P("mp", None),
            P(),
            P(None, "mp"),
            P(None, "mp"),
            P("mp", None),
        ),
        out_specs=(P(("req", "mp"), None), P("req", None, "mp", None)),
        check_vma=False,
    )
```

time: 274 us -> 116 us (0.42)
  waiting for transfers between devices: 182 us -> 0 us
  Pallas kernels: 11.7 us -> 107 us
  matrix products: 27.5 us -> 0 us
  other arithmetic: 20 us -> 2.44 us
  between operations: 14 us -> 0.69 us
  local copies, waits for them, and re-layouts: 16 us -> 5.14 us
    all_gather x3 -> x0, waiting for transfers between devices: 131 us -> none  [the longest x1 72.4 us: body(): everything = lax.all_gather(pairs, 'req', axis=0, tiled=True)]
    pallas_call x0 -> x1, Pallas kernels: none -> 95.7 us  [run_layer(): pl.pallas_call(layer_kernel, out_shape=(jax.ShapeDtypeStruct((rows, width...]
    reduce_scatter x2 -> x0, waiting for transfers between devices: 49.5 us -> none  [the longest x1 29.8 us: body(): lax.psum_scatter(jnp.dot(attended, w_out, preferred_element_type=jnp.floa...]
    dot_general x8 -> x0, matrix products: 27.5 us -> none  [the longest x1 8.31 us: body(): jnp.dot(hidden, w_down, preferred_element_type=jnp.float32)]
    another operation x4 -> x0, local copies, waits for them, and re-layouts: 7.08 us -> none
    convert_element_type x7 -> x0, other arithmetic: 6.25 us -> none  [the longest x1 2.12 us: body(): after = (hidden_in.astype(jnp.float32) + own_sum).astype(jnp.bfloat16)]
    reduce_sum x4 -> x0, other arithmetic: 4.35 us -> none  [the longest x2 4.15 us: rms_scale(): jnp.mean(wide * wide, axis=-1, keepdims=True) + EPS]
    reshape x2 -> x0, local copies, waits for them, and re-layouts: 3.86 us -> none  [the longest x1 2.04 us: body(): jnp.dot(normed, w_key, preferred_element_type=jnp.float32)]
  transfers between devices with their start and end apart: 5 -> 0, of which waited for: 5 -> 0; matrix products, arithmetic and copies ran while one was open for 7% -> 0% of each run, Pallas kernels for 0% -> 0%
where the time goes in v2:
time: 116 us
  Pallas kernels  107 us (92%)
  local copies, waits for them, and re-layouts  5.14 us (4%)
  other arithmetic  2.44 us (2%)
    pallas_call x1, Pallas kernels, run_layer(): pl.pallas_call(layer_kernel, out_shape=(jax.ShapeDtypeStruct((rows, width...  95.7 us
    pallas_call x1, Pallas kernels, fill_pages(): pl.pallas_call(fill_kernel, out_shape=jax.ShapeDtypeStruct((requests * mo...  11.7 us

profile of v2, /device:TPU:0, one launch (start us, length us, event | category | flops | bytes accessed | tf_op | source)
XLA Modules:
  0.0 115.7 jit_solution(16201500028460127961)
XLA Ops:
  0.6 1.0 convert_reduce_fusion
  1.6 1.3 %broadcast_in_dim.39.ln_attn = bf16[1,2048]{1,0:T(2,128)(2,1)} reshape(bf16[2048]{0:T(1024)(128)(2,1)} %param.19) | data formatting | bytes 8192 | tf_op jit(solution)/shard_map/broadcast_in_dim | solution.py:568
  2.9 1.3 %broadcast_in_dim.42.ln_mlp = bf16[1,2048]{1,0:T(2,128)(2,1)} reshape(bf16[2048]{0:T(1024)(128)(2,1)} %param.26) | data formatting | bytes 8192 | tf_op jit(solution)/shard_map/broadcast_in_dim | solution.py:575
  4.2 0.1 copy.19
  4.3 0.1 broadcast_in_dim.43
  4.4 0.1 copy.20
  4.5 0.1 broadcast_in_dim.46
  4.6 1.4 %select_reduce_fusion = (s32[32]{0:T(128)}, s32[32]{0:T(128)}) fusion(s32[96]{0:T(128)S(1)} %broadcast_in_dim.46, s32[32]{0:T(128)} %param.17, s32[96]{0:T(128)S(1)} %broadcast_in_dim.43), kind=kLoop, calls=%fused_computation.2 | loop fusion | flops 15296 | bytes 1152 | tf_op jit(solution)/shard_map/reduce_sum | solution.py:27
  6.1 1.4 %copy.21.table_ref = s32[32,16]{1,0:T(8,128)} copy(s32[32,16]{0,1:T(8,128)} %param.18) | data formatting | bytes 4096 | tf_op args[3]
  7.4 95.7 %layer.1 = (bf16[128,2048]{1,0:T(8,128)(2,1)}, bf16[16384,2,256]{2,1,0:T(2,128)(2,1)}) custom-call(bf16[128,2048]{1,0:T(8,128)(2,1)} %hidden.1, s32[32,512]{1,0:T(8,128)} %seg.1, bf16[1,2048]{1,0:T(2,128)(2,1)} %broadcast_in_dim.39.ln_attn, bf16[2048,512]{1,0:T(8,128)(2,1)} %w_query.1, bf16[2048,256]{1,0:T(8,128)(2,1)} %w_key.1, bf16[2048,256]{1,0:T(8,128)(2,1)} %w_value.1, ...), custom_call_target="tpu_custom_call" | custom-call | tf_op jit(solution)/shard_map/layer/pallas_call | solution.py:506
  103.2 0.0 copy-start
  103.2 11.7 %fill_pages.1 = bf16[512,16,2,256]{3,2,1,0:T(2,128)(2,1)} custom-call(s32[32]{0:T(128)} %get-tuple-element.7.begin_ref, s32[32]{0:T(128)} %get-tuple-element.6.length_ref, s32[32,16]{1,0:T(8,128)} %copy.21.table_ref, bf16[16384,2,256]{2,1,0:T(2,128)(2,1)} %get-tuple-element.5.rows_ref), custom_call_target="tpu_custom_call" | custom-call | tf_op jit(solution)/shard_map/fill_pages/pallas_call | solution.py:102
  114.9 0.0 copy-done
  114.9 0.8 copy.23
  (2 shorter events, 0.0 us)
Async XLA Ops:
  103.2 11.7 %copy-start = (bf16[128,2048]{1,0:T(8,128)(2,1)S(1)}, bf16[128,2048]{1,0:T(8,128)(2,1)}, u32[]{:S(2)}) copy-start(bf16[128,2048]{1,0:T(8,128)(2,1)} %get-tuple-element.12) | copy-start | bytes 1572868

commit v3 on v2

--- a/solution.py
+++ b/solution.py
@@ -16,29 +16,43 @@
 THETA = 1000000.0
 
 
-def request_rows(segment_ids, request_prompt, seq_rows):
-    bound = jnp.arange(PROMPTS_DEV + 1, dtype=jnp.int32)
-    below = jnp.sum((segment_ids[:, None, :] < bound[None, :, None]).astype(jnp.int32), axis=2)
-    groups = segment_ids.shape[0]
-    first = below[:, :PROMPTS_DEV] + jnp.arange(groups, dtype=jnp.int32)[:, None] * seq_rows
-    counts = below[:, 1:] - below[:, :-1]
-    picks = request_prompt[:, None] == jnp.arange(groups * PROMPTS_DEV, dtype=jnp.int32)[None, :]
-    begin = jnp.sum(jnp.where(picks, first.reshape(-1)[None, :], 0), axis=1)
-    length = jnp.sum(jnp.where(picks, counts.reshape(-1)[None, :], 0), axis=1)
-    return begin, length
-
-
-SLOTS = 8
-
-
-def fill_kernel(begin_ref, length_ref, table_ref, rows_ref, out_ref, slots, zeros, in_sem, out_sem):
-    requests, most = table_ref.shape
+SLOTS = 16
+AHEAD = 12
+
+
+def fill_kernel(
+    table_hbm, prompt_hbm, bounds_hbm, layer_hbm, rows_ref, out_ref, layer_out, table, prompt, bounds, held, slots,
+    zeros, small_sem, in_sem, out_sem,
+):
+    most, requests = table.shape
     span = most * PAGE
     last = rows_ref.shape[0] - span
+    seq = rows_ref.shape[0] // bounds.shape[0]
+    smalls = [
+        pltpu.make_async_copy(src, dst, small_sem.at[n])
+        for n, (src, dst) in enumerate(
+            ((table_hbm, table), (prompt_hbm, prompt), (bounds_hbm, bounds), (layer_hbm, held))
+        )
+    ]
+    layer_copy = pltpu.make_async_copy(held, layer_out, small_sem.at[4])
+    for small in smalls:
+        small.start()
     zeros[...] = jnp.zeros_like(zeros)
+    for small in smalls:
+        small.wait()
+    layer_copy.start()
+
+    def place(r):
+        p = prompt[r]
+        g = p // PROMPTS_DEV
+        s = p - g * PROMPTS_DEV
+        low = jnp.where(s == 0, 0, jnp.where(s == 1, bounds[g, 0], bounds[g, 1]))
+        high = jnp.where(s == 0, bounds[g, 0], jnp.where(s == 1, bounds[g, 1], seq))
+        begin = g * seq + low
+        return begin, high - low, jnp.minimum(begin, last)
 
     def fetch(r, slot):
-        at = jnp.minimum(begin_ref[r], last)
+        at = place(r)[2]
         return pltpu.make_async_copy(
             rows_ref.at[pl.ds(at, span)], slots.at[slot, pl.ds(0, span)], in_sem.at[slot]
         )
@@ -48,28 +62,27 @@
             out_ref.at[pl.ds(0, most)], out_ref.at[pl.ds(0, most)], out_sem.at[slot]
         ).wait()
 
-    ahead = SLOTS // 2
-    for r in range(ahead):
+    for r in range(min(AHEAD, requests)):
         fetch(r, r).start()
 
     @pl.loop(0, requests)
     def _(r):
         slot = lax.rem(r, SLOTS)
         fetch(r, slot).wait()
-        begin, length = begin_ref[r], length_ref[r]
-        shift = begin - jnp.minimum(begin, last)
+        begin, length, at = place(r)
+        shift = begin - at
         full = length // PAGE
         rest = length - full * PAGE
 
         @pl.when(rest > 0)
         def _():
-            at = shift + full * PAGE
-            tail = slots[slot, pl.ds(at, PAGE)]
+            edge = shift + full * PAGE
+            tail = slots[slot, pl.ds(edge, PAGE)]
             row = lax.broadcasted_iota(jnp.int32, tail.shape, 0)
-            slots[slot, pl.ds(at, PAGE)] = jnp.where(row < rest, tail, jnp.zeros_like(tail))
+            slots[slot, pl.ds(edge, PAGE)] = jnp.where(row < rest, tail, jnp.zeros_like(tail))
 
         for e in range(most):
-            page = table_ref[r, e]
+            page = table[e, r]
 
             @pl.when(e * PAGE < length)
             def _():
@@ -81,37 +94,46 @@
             def _():
                 pltpu.make_async_copy(zeros, out_ref.at[page], out_sem.at[slot]).start()
 
-        @pl.when(r + ahead < requests)
+        @pl.when(r + AHEAD < requests)
         def _():
-            other = lax.rem(r + ahead, SLOTS)
-
-            @pl.when(r + ahead >= SLOTS)
+            other = lax.rem(r + AHEAD, SLOTS)
+
+            @pl.when(r + AHEAD >= SLOTS)
             def _():
                 drain(other)
 
-            fetch(r + ahead, other).start()
+            fetch(r + AHEAD, other).start()
 
     for r in range(max(0, requests - SLOTS), requests):
         drain(r % SLOTS)
-
-
-def fill_pages(begin, length, page_table, rows):
+    layer_copy.wait()
+
+
+def fill_pages(page_table, request_prompt, bounds, layer, rows):
     requests, most = page_table.shape
     unit = rows.shape[1:]
-    smem = pl.BlockSpec(memory_space=pltpu.SMEM)
+    hbm = pl.BlockSpec(memory_space=pl.ANY)
     return pl.pallas_call(
         fill_kernel,
-        out_shape=jax.ShapeDtypeStruct((requests * most, PAGE) + unit, rows.dtype),
-        in_specs=[smem, smem, smem, pl.BlockSpec(memory_space=pl.ANY)],
-        out_specs=pl.BlockSpec(memory_space=pl.ANY),
+        out_shape=(
+            jax.ShapeDtypeStruct((requests * most, PAGE) + unit, rows.dtype),
+            jax.ShapeDtypeStruct(layer.shape, layer.dtype),
+        ),
+        in_specs=[hbm] * 5,
+        out_specs=(hbm, hbm),
         scratch_shapes=[
+            pltpu.SMEM((most, requests), jnp.int32),
+            pltpu.SMEM((requests,), jnp.int32),
+            pltpu.SMEM(bounds.shape, jnp.int32),
+            pltpu.VMEM(layer.shape, layer.dtype),
             pltpu.VMEM((SLOTS, (most + 1) * PAGE) + unit, rows.dtype),
             pltpu.VMEM((PAGE,) + unit, rows.dtype),
+            pltpu.SemaphoreType.DMA((5,)),
             pltpu.SemaphoreType.DMA((SLOTS,)),
             pltpu.SemaphoreType.DMA((SLOTS,)),
         ],
         name="fill_pages",
-    )(begin, length, page_table, rows)
+    )(page_table.T, request_prompt, bounds, layer, rows)
 
 
 MESH = pl.DeviceIdType.MESH
@@ -142,6 +164,7 @@
     w_down,
     out,
     kv,
+    bounds,
     hbuf,
     abuf,
     wq,
@@ -245,9 +268,13 @@
             own = hidden.at[pl.ds(d * HALF + p * sub, sub)]
             remote(own, hbuf.at[x, d, p], ag1_send.at[0, d, p], ag1_recv.at[0, d, p], x_near[d]).start()
 
+    def below(table, bound):
+        return jnp.sum((table < bound).astype(jnp.int32), axis=1, keepdims=True)
+
     seg_row = seg[pl.ds(c, 1), :]
-    first1 = jnp.sum((seg_row < 1).astype(jnp.int32), axis=1, keepdims=True)
-    first2 = jnp.sum((seg_row < 2).astype(jnp.int32), axis=1, keepdims=True)
+    first1, first2 = below(seg_row, 1), below(seg_row, 2)
+    place = lax.broadcasted_iota(jnp.int32, bounds.shape, 1)
+    bounds[...] = jnp.where(place == 0, below(seg[...], 1), below(seg[...], 2))
 
     def begin_of(token):
         return jnp.where(token >= first2, first2, jnp.where(token >= first1, first1, 0))
@@ -255,10 +282,9 @@
     lane = lax.broadcasted_iota(jnp.int32, (1, HD), 1)
     freq = jnp.exp2(lax.rem(lane, HD // 2).astype(jnp.float32) * (-2.0 * math.log2(THETA) / HD))
     sign = jnp.where(lane < HD // 2, -1.0, 1.0)
-    gain_attn = ln_attn[...].astype(jnp.float32)
-    gain_mlp = ln_mlp[...].astype(jnp.float32)
-    gain_q = q_gain[...].astype(jnp.float32)
-    gain_k = k_gain[...].astype(jnp.float32)
+    gain_attn, gain_mlp, gain_q, gain_k = (
+        gain[...].astype(jnp.float32).reshape(1, -1) for gain in (ln_attn, ln_mlp, q_gain, k_gain)
+    )
     heads = wq.shape[1] // HD
     kv_heads = wk.shape[1] // HD
     group = heads // kv_heads
@@ -370,8 +396,6 @@
                 at = (n * group + h) * HD
                 attbuf[i, 0, :, at : at + HD] = mixed[h * rows : h * rows + HALF]
                 attbuf[i, 1, :, at : at + HD] = mixed[h * rows + HALF : (h + 1) * rows]
-    pump(jnp.int32(1))
-
     piece = width // SUBS
 
     def sum_step(send_buf, recv_buf, send, recv, j, d, n):
@@ -402,6 +426,7 @@
     mixed = out_rows(0)
     for n in range(SUBS):
         send_on(out_part(mixed, n), *ring1, 0, n)
+    pump(jnp.int32(1))
 
     @pl.loop(1, SIDE - 1)
     def _(j):
@@ -412,6 +437,8 @@
             send_on(part, *ring1, j, n)
         pump(j + 1)
 
+    pump(jnp.int32(SIDE))
+    pump(jnp.int32(SIDE + 1))
     mixed = out_rows(SIDE - 1)
     for n in range(SUBS):
         part = add_arrived(out_part(mixed, n), *ring1, SIDE - 2, n)
@@ -422,7 +449,8 @@
     for p in range(SUBS):
         for d in range(2):
             gather_step(abuf, ag2_send, ag2_recv, 0, d, p).start()
-    pump(jnp.int32(SIDE))
+    pump(jnp.int32(SIDE + 2))
+    pump(jnp.int32(SIDE + 3))
 
     for move in moves[2 * SUBS + 4 :]:
         move.wait()
@@ -443,7 +471,7 @@
             gather_advance(abuf, ag2_send, ag2_recv, j)
 
         actbuf[...] = activation(j)
-        pump(2 * j + SIDE + 1)
+        pump(2 * j + 2 * SIDE)
 
         @pl.when(j > 0)
         def _():
@@ -462,11 +490,9 @@
         def _():
             ownbuf[...] = actbuf[...]
 
-        pump(2 * j + SIDE + 2)
+        pump(2 * j + 2 * SIDE + 1)
 
     act = ownbuf[...]
-    for p in range(3 * SIDE + 1, PUMPS):
-        pump(jnp.int32(p))
     for n in range(SUBS):
         part = add_arrived(down_part(act, n), *ring2, SIDE - 2, n)
         for d in range(2):
@@ -508,9 +534,10 @@
         out_shape=(
             jax.ShapeDtypeStruct((rows, width), bf16),
             jax.ShapeDtypeStruct((seg.shape[0] * seq, kvw // HD, 2 * HD), bf16),
+            jax.ShapeDtypeStruct((seg.shape[0], HD), jnp.int32),
         ),
         in_specs=[hbm, vmem, vmem, hbm, hbm, hbm, vmem, vmem, hbm, vmem, hbm, hbm, hbm],
-        out_specs=(vmem, hbm),
+        out_specs=(vmem, hbm, vmem),
         scratch_shapes=[
             pltpu.VMEM((SIDE, 2, SUBS, sub, width), bf16),
             pltpu.VMEM((SIDE, 2, SUBS, sub, width), bf16),
@@ -561,23 +588,23 @@
     w_up,
     w_down,
 ):
-    begin, length = request_rows(segment_ids, request_prompt, segment_ids.shape[1])
-    result, everything = run_layer(
+    result, everything, bounds = run_layer(
         hidden_in,
         segment_ids,
-        ln_attn[None, :],
+        ln_attn,
         w_query,
         w_key,
         w_value,
-        q_gain[None, :],
-        k_gain[None, :],
+        q_gain,
+        k_gain,
         w_out,
-        ln_mlp[None, :],
+        ln_mlp,
         w_gate,
         w_up,
         w_down,
     )
-    return (result, fill_pages(begin, length, page_table, everything))
+    cache, result = fill_pages(page_table, request_prompt, bounds, result, everything)
+    return (result, cache)
 
 
 def solution(mesh):

time: 116 us -> 98.7 us (0.85)
  Pallas kernels: 107 us -> 97.7 us
  local copies, waits for them, and re-layouts: 5.14 us -> 0 us
  other arithmetic: 2.44 us -> 0 us
    pallas_call x1, Pallas kernels: 95.7 us -> 89.7 us  [run_layer(): pl.pallas_call(layer_kernel, out_shape=(jax.ShapeDtypeStruct((rows, width...]
    pallas_call x1, Pallas kernels: 11.7 us -> 8.01 us  [fill_pages(): pl.pallas_call(fill_kernel, out_shape=(jax.ShapeDtypeStruct((requests * m...]
    broadcast_in_dim x4 -> x0, local copies, waits for them, and re-layouts: 2.79 us -> none  [the longest x1 1.29 us: body(): ln_attn[None, :]]
    reduce_sum x2 -> x0, other arithmetic: 2.43 us -> none  [the longest x1 1.44 us: request_rows(): length = jnp.sum(jnp.where(picks, counts.reshape(-1)[None, :], 0), axis=1)]
    unnamed x4 -> x0, local copies, waits for them, and re-layouts: 2.18 us -> none
where the time goes in v3:
time: 98.7 us; the launch traced here: 98.4 us
  Pallas kernels  97.7 us (99%)
    pallas_call x1, Pallas kernels, run_layer(): pl.pallas_call(layer_kernel, out_shape=(jax.ShapeDtypeStruct((rows, width...  89.7 us
    pallas_call x1, Pallas kernels, fill_pages(): pl.pallas_call(fill_kernel, out_shape=(jax.ShapeDtypeStruct((requests * m...  8.01 us

profile of v3, /device:TPU:0, one launch (start us, length us, event | category | flops | bytes accessed | tf_op | source)
XLA Modules:
  0.0 98.4 jit_solution(5301457359278466268)
XLA Ops:
  0.6 89.7 %layer.1 = (bf16[128,2048]{1,0:T(8,128)(2,1)}, bf16[16384,2,256]{2,1,0:T(2,128)(2,1)}, s32[32,128]{1,0:T(8,128)}) custom-call(bf16[128,2048]{1,0:T(8,128)(2,1)} %hidden.1, s32[32,512]{1,0:T(8,128)} %seg.1, bf16[2048]{0:T(1024)(128)(2,1)} %ln_attn.1, bf16[2048,512]{1,0:T(8,128)(2,1)} %w_query.1, bf16[2048,256]{1,0:T(8,128)(2,1)} %w_key.1, ...), custom_call_target="tpu_custom_call" | custom-call | tf_op jit(solution)/shard_map/layer/pallas_call | solution.py:532
  90.4 8.0 %fill_pages.1 = (bf16[512,16,2,256]{3,2,1,0:T(2,128)(2,1)}, bf16[128,2048]{1,0:T(8,128)(2,1)}) custom-call(s32[16,32]{1,0:T(8,128)} %bitcast.1, s32[32]{0:T(128)} %prompt_hbm.1, s32[32,128]{1,0:T(8,128)} %get-tuple-element.7.bounds_hbm, bf16[128,2048]{1,0:T(8,128)(2,1)} %get-tuple-element.8.layer_hbm, bf16[16384,2,256]{2,1,0:T(2,128)(2,1)} %get-tuple-element.9.rows_ref), custom_call_target="tpu_custom_call" | custom-call | tf_op jit(solution)/shard_map/fill_pages/pallas_call | solution.py:116

commit v4 on v3

--- a/solution.py
+++ b/solution.py
@@ -182,15 +182,22 @@
     actbuf,
     ownbuf,
     send2f,
-    send1,
-    recv1,
+    wfull,
+    att_in,
+    relay,
     send2,
     recv2,
     local_sem,
     ag1_send,
     ag1_recv,
-    rs1_send,
-    rs1_recv,
+    wx_send,
+    wx_recv,
+    a_send,
+    a_recv,
+    w_send,
+    w1_recv,
+    w2_recv,
+    w_pair_recv,
     ag2_send,
     ag2_recv,
     rs2_send,
@@ -235,9 +242,10 @@
         move.start()
 
     barrier = pltpu.get_barrier_semaphore()
-    for near in x_near + y_near + z_near + (pair,):
+    peers = x_near + y_near + z_near + (pair, (c, turn(x + 2)))
+    for near in peers:
         pl.semaphore_signal(barrier, inc=1, device_id=near, device_id_type=MESH)
-    pl.semaphore_wait(barrier, 7)
+    pl.semaphore_wait(barrier, len(peers))
 
     def remote(src, dst, send, recv, near):
         return pltpu.make_async_remote_copy(
@@ -248,14 +256,13 @@
         block = buf.at[turn(x - j) if d == 0 else turn(x + j), d, p]
         return remote(block, block, send.at[j, d, p], recv.at[j, d, p], x_near[d])
 
-    def gather_advance(buf, send, recv, j):
-        for p in range(SUBS):
-            for d in range(2):
-                gather_step(buf, send, recv, j - 1, d, p).wait_recv()
-
-                @pl.when(j < SIDE - 1)
-                def _():
-                    gather_step(buf, send, recv, j, d, p).start()
+    def gather_advance(buf, send, recv, j, p):
+        for d in range(2):
+            gather_step(buf, send, recv, j - 1, d, p).wait_recv()
+
+            @pl.when(j < SIDE - 1)
+            def _():
+                gather_step(buf, send, recv, j, d, p).start()
 
     def ring_rows(buf, j):
         a, b = turn(x - j), turn(x + j)
@@ -263,6 +270,19 @@
         lower = buf[b, 1].reshape(HALF, width)
         return jnp.concatenate([upper, lower], axis=0).astype(jnp.float32)
 
+    deep = wfull.shape[4]
+
+    def out_exchange(k):
+        return remote(
+            w_out.at[pl.ds(c * deep, deep)],
+            wfull.at[k - 1, y, z, core],
+            wx_send.at[k - 1],
+            wx_recv.at[k - 1],
+            (c, turn(x - k)),
+        )
+
+    for k in (2, 1, 3):
+        out_exchange(k).start()
     for p in range(SUBS):
         for d in range(2):
             own = hidden.at[pl.ds(d * HALF + p * sub, sub)]
@@ -289,6 +309,57 @@
     kv_heads = wk.shape[1] // HD
     group = heads // kv_heads
 
+    flows = ((0, 0), (0, 1), (1, 0), (1, 1))
+
+    def make_pump(block_of, send, recv1, recv2, pair_recv):
+        def pump(p):
+            b, k = lax.rem(p, SIDE), p // SIDE
+            for f, (axis, d) in enumerate(flows):
+                step = 1 if d == 0 else -1
+                first = y_near[d] if axis == 0 else z_near[d]
+                second = z_near[d] if axis == 0 else y_near[d]
+                if axis == 0:
+                    block = block_of(f, turn(y - step * b), turn(z - step * k))
+                else:
+                    block = block_of(f, turn(y - step * k), turn(z - step * b))
+
+                @pl.when((p >= 1) & (p < SIDE))
+                def _():
+                    remote(block, block, send.at[0], recv1.at[f, p - 1], first).wait_recv()
+
+                @pl.when(p >= SIDE)
+                def _():
+                    remote(block, block, send.at[1], recv2.at[f, p - SIDE], second).wait_recv()
+
+                @pl.when(p < SIDE - 1)
+                def _():
+                    remote(block, block, send.at[0], recv1.at[f, p], first).start()
+
+                @pl.when(p < PUMPS - SIDE)
+                def _():
+                    remote(block, block, send.at[1], recv2.at[f, p], second).start()
+
+                remote(block, block, send.at[2], pair_recv.at[0], pair).start()
+
+        return pump
+
+    seq = SIDE * rows
+    strip = width // len(flows)
+
+    def kv_block(f, oy, oz):
+        return kv.at[pl.ds(pl.multiple_of(req_of(oy, oz, core) * seq + f * UNIT, UNIT), UNIT)]
+
+    def w_block(f, oy, oz):
+        return wfull.at[:, oy, oz, core, :, pl.ds(f * strip, strip)]
+
+    pump = make_pump(kv_block, kv_send, kv1_recv, kv2_recv, kv_pair_recv)
+    w_pump = make_pump(w_block, w_send, w1_recv, w2_recv, w_pair_recv)
+
+    def settle(send, pair_recv, first, second, last):
+        remote(first, first, send.at[0], pair_recv.at[0], pair).wait_send()
+        remote(second, second, send.at[1], pair_recv.at[0], pair).wait_send()
+        remote(last, last, send.at[2], pair_recv.at[0], pair).wait_send()
+
     for move in moves[: 2 * SUBS + 3]:
         move.wait()
 
@@ -296,7 +367,9 @@
     def _(j):
         @pl.when(j > 0)
         def _():
-            gather_advance(hbuf, ag1_send, ag1_recv, j)
+            for p in range(SUBS):
+                gather_advance(hbuf, ag1_send, ag1_recv, j, p)
+                w_pump(3 * j - 2 + p)
 
         a, b = turn(x - j), turn(x + j)
         normed = rms(ring_rows(hbuf, j), gain_attn).astype(jnp.bfloat16)
@@ -328,45 +401,33 @@
         vbuf[a, 0] = value[:HALF]
         vbuf[b, 1] = value[HALF:]
 
-    seq = SIDE * rows
+        @pl.when(j == 0)
+        def _():
+            for k in (1, 3, 2):
+                out_exchange(k).wait_recv()
+
+        w_pump(3 * j)
+
     kv_own = pltpu.make_async_copy(kvbuf, kv.at[pl.ds(c * seq, seq)], local_sem.at[2 * SUBS + len(weights)])
     kv_own.start()
 
-    flows = ((0, 0), (0, 1), (1, 0), (1, 1))
-
-    def pump(p):
-        b, k = lax.rem(p, SIDE), p // SIDE
-        for f, (axis, d) in enumerate(flows):
-            sign_d = 1 if d == 0 else -1
-            first = y_near[d] if axis == 0 else z_near[d]
-            second = z_near[d] if axis == 0 else y_near[d]
-            if axis == 0:
-                oy, oz = turn(y - sign_d * b), turn(z - sign_d * k)
-            else:
-                oy, oz = turn(y - sign_d * k), turn(z - sign_d * b)
-            at = req_of(oy, oz, core) * seq + f * UNIT
-            block = kv.at[pl.ds(pl.multiple_of(at, UNIT), UNIT)]
-
-            @pl.when((p >= 1) & (p < SIDE))
-            def _():
-                remote(block, block, kv_send.at[0], kv1_recv.at[f, p - 1], first).wait_recv()
-
-            @pl.when(p >= SIDE)
-            def _():
-                remote(block, block, kv_send.at[0], kv2_recv.at[f, p - SIDE], second).wait_recv()
-
-            @pl.when(p < SIDE - 1)
-            def _():
-                remote(block, block, kv_send.at[0], kv1_recv.at[f, p], first).start()
-
-            @pl.when(p < PUMPS - SIDE)
-            def _():
-                remote(block, block, kv_send.at[0], kv2_recv.at[f, p], second).start()
-
-            remote(block, block, kv_send.at[0], kv_pair_recv.at[0], pair).start()
-
+    w_pump(jnp.int32(3 * SIDE - 2))
+    w_pump(jnp.int32(3 * SIDE - 1))
     kv_own.wait()
     pump(jnp.int32(0))
+
+    def a_copy(n, src, dst, near):
+        return remote(src, dst, a_send.at[n], a_recv.at[n], near)
+
+    def head_copy(n, i=0):
+        if n < 2:
+            return a_copy(n, attbuf.at[i], att_in.at[2 - 2 * n], x_near[n])
+        return a_copy(n, attbuf.at[i, n - 2], relay.at[n - 2], x_near[n - 2])
+
+    relays = (
+        a_copy(4, relay.at[0], att_in.at[1, 0], x_near[0]),
+        a_copy(5, relay.at[1], att_in.at[1, 1], x_near[1]),
+    )
 
     keys = kbuf[...].reshape(seq, kv_heads * HD)
     values = vbuf[...].reshape(seq, kv_heads * HD)
@@ -396,6 +457,22 @@
                 at = (n * group + h) * HD
                 attbuf[i, 0, :, at : at + HD] = mixed[h * rows : h * rows + HALF]
                 attbuf[i, 1, :, at : at + HD] = mixed[h * rows + HALF : (h + 1) * rows]
+        ahead = turn(i - x)
+
+        @pl.when(ahead == 1)
+        def _():
+            head_copy(0, i).start()
+
+        @pl.when(ahead == SIDE - 1)
+        def _():
+            head_copy(1, i).start()
+
+        @pl.when(ahead == 2)
+        def _():
+            head_copy(2, i).start()
+            head_copy(3, i).start()
+
+        w_pump(jnp.int32(3 * SIDE + i))
     piece = width // SUBS
 
     def sum_step(send_buf, recv_buf, send, recv, j, d, n):
@@ -412,45 +489,44 @@
             send_buf[j, d, n] = rounded[d * HALF : (d + 1) * HALF]
             sum_step(send_buf, recv_buf, send, recv, j, d, n).start()
 
-    ring1 = (send1, recv1, rs1_send, rs1_recv)
     ring2 = (send2, recv2, rs2_send, rs2_recv)
 
+    def add_heads(mixed, weight, n):
+        send2f[n] += jnp.dot(mixed, weight, preferred_element_type=jnp.float32)
+
+    def add_source(k):
+        mixed = att_in[k - 1].reshape(rows, att_in.shape[3])
+        for n in range(SUBS):
+            weight = wfull[k - 1, :, :, :, :, n * piece : (n + 1) * piece].reshape(att_in.shape[3], piece)
+            add_heads(mixed, weight, n)
+
     moves[2 * SUBS + 3].wait()
-
-    def out_rows(j):
-        return jnp.concatenate([attbuf[turn(x - 1 - j), 0], attbuf[turn(x + 1 + j), 1]], axis=0)
-
-    def out_part(mixed, n):
-        return jnp.dot(mixed, wo[:, n * piece : (n + 1) * piece], preferred_element_type=jnp.float32)
-
-    mixed = out_rows(0)
+    for n, move in enumerate(relays):
+        head_copy(2 + n).wait_recv()
+        move.start()
+    mixed = attbuf[x].reshape(rows, heads * HD)
     for n in range(SUBS):
-        send_on(out_part(mixed, n), *ring1, 0, n)
-    pump(jnp.int32(1))
-
-    @pl.loop(1, SIDE - 1)
-    def _(j):
-        mixed = out_rows(j)
-        for n in range(SUBS):
-            part = out_part(mixed, n)
-            part = add_arrived(part, *ring1, j - 1, n)
-            send_on(part, *ring1, j, n)
-        pump(j + 1)
-
-    pump(jnp.int32(SIDE))
-    pump(jnp.int32(SIDE + 1))
-    mixed = out_rows(SIDE - 1)
+        columns = slice(n * piece, (n + 1) * piece)
+        before = [hbuf[x, d, :, :, columns].reshape(HALF, piece) for d in range(2)]
+        send2f[n] = jnp.concatenate(before, axis=0).astype(jnp.float32)
+        add_heads(mixed, wo[:, columns], n)
+    half = wfull.at[:, :, :, 0]
+    remote(half, half, w_send.at[2], w_pair_recv.at[0], pair).wait_recv()
+    head_copy(1).wait_recv()
+    add_source(1)
+    head_copy(0).wait_recv()
+    add_source(3)
+    for move in relays:
+        move.wait_recv()
+    add_source(2)
     for n in range(SUBS):
-        part = add_arrived(out_part(mixed, n), *ring1, SIDE - 2, n)
+        total = send2f[n].astype(jnp.bfloat16)
         for d in range(2):
-            before = hbuf[x, d, :, :, n * piece : (n + 1) * piece].astype(jnp.float32)
-            total = before + part[d * HALF : (d + 1) * HALF].reshape(SUBS, sub, piece)
-            abuf[x, d, :, :, n * piece : (n + 1) * piece] = total.astype(jnp.bfloat16)
+            abuf[x, d, :, :, n * piece : (n + 1) * piece] = total[d * HALF : (d + 1) * HALF].reshape(SUBS, sub, piece)
     for p in range(SUBS):
         for d in range(2):
             gather_step(abuf, ag2_send, ag2_recv, 0, d, p).start()
-    pump(jnp.int32(SIDE + 2))
-    pump(jnp.int32(SIDE + 3))
+    pump(jnp.int32(1))
 
     for move in moves[2 * SUBS + 4 :]:
         move.wait()
@@ -468,10 +544,15 @@
     def _(j):
         @pl.when(j > 0)
         def _():
-            gather_advance(abuf, ag2_send, ag2_recv, j)
+            for p in range(SUBS):
+                gather_advance(abuf, ag2_send, ag2_recv, j, p)
+                pump(4 * j - 1 + p)
 
         actbuf[...] = activation(j)
-        pump(2 * j + 2 * SIDE)
+
+        @pl.when(j > 0)
+        def _():
+            pump(4 * j + 1)
 
         @pl.when(j > 0)
         def _():
@@ -490,9 +571,10 @@
         def _():
             ownbuf[...] = actbuf[...]
 
-        pump(2 * j + 2 * SIDE + 1)
+        pump(4 * j + 2)
 
     act = ownbuf[...]
+    pump(jnp.int32(PUMPS - 1))
     for n in range(SUBS):
         part = add_arrived(down_part(act, n), *ring2, SIDE - 2, n)
         for d in range(2):
@@ -506,14 +588,26 @@
             for p in range(SUBS):
                 gather_step(hbuf, ag1_send, ag1_recv, j, d, p).wait_send()
                 gather_step(abuf, ag2_send, ag2_recv, j, d, p).wait_send()
-                sum_step(*ring1, j, d, p).wait_send()
                 sum_step(*ring2, j, d, p).wait_send()
 
-    sent = UNIT * len(flows) * (SIDE - 1 + PUMPS - SIDE + PUMPS)
-    whole = kv.at[pl.ds(0, sent)]
-    remote(whole, whole, kv_send.at[0], kv_pair_recv.at[0], pair).wait_send()
+    for k in range(1, SIDE):
+        out_exchange(k).wait_send()
+    for n in range(4):
+        head_copy(n).wait_send()
+    for move in relays:
+        move.wait_send()
+    settle(
+        w_send, w_pair_recv, wfull.at[:, 0, pl.ds(0, SIDE - 1), 0], wfull.at[:, pl.ds(0, SIDE - 1), :, 0], half
+    )
+    settle(
+        kv_send,
+        kv_pair_recv,
+        kv.at[pl.ds(0, UNIT * len(flows) * (SIDE - 1))],
+        kv.at[pl.ds(0, UNIT * len(flows) * (PUMPS - SIDE))],
+        kv.at[pl.ds(0, UNIT * len(flows) * PUMPS)],
+    )
     got = kv.at[pl.ds(0, UNIT * len(flows) * PUMPS)]
-    remote(got, got, kv_send.at[0], kv_pair_recv.at[0], pair).wait_recv()
+    remote(got, got, kv_send.at[2], kv_pair_recv.at[0], pair).wait_recv()
 
 
 def run_layer(hidden, seg, ln_attn, w_query, w_key, w_value, q_gain, k_gain, w_out, ln_mlp, w_gate, w_up, w_down):
@@ -528,6 +622,7 @@
     hbm = pl.BlockSpec(memory_space=pl.ANY)
     ring = (SIDE - 1, 2, SUBS)
     dma = pltpu.SemaphoreType.DMA
+    gather_sems = [dma((3,)), dma((4, SIDE - 1)), dma((4, PUMPS - SIDE)), dma((1,))]
     blocks = pltpu.VMEM(ring + (HALF, width // SUBS), bf16)
     return pl.pallas_call(
         layer_kernel,
@@ -556,14 +651,22 @@
             pltpu.VMEM((rows, units), bf16),
             pltpu.VMEM((rows, units), bf16),
             pltpu.VMEM((SUBS, rows, width // SUBS), f32),
-            blocks,
-            blocks,
+            pltpu.VMEM((SIDE - 1, SIDE, SIDE, 2, w_out.shape[0] // seg.shape[0], width), bf16),
+            pltpu.VMEM((SIDE - 1, 2, HALF, heads_w), bf16),
+            pltpu.VMEM((2, HALF, heads_w), bf16),
             blocks,
             blocks,
             dma((2 * SUBS + 8,)),
+            dma(ring),
+            dma(ring),
+            dma((SIDE - 1,)),
+            dma((SIDE - 1,)),
+            dma((6,)),
+            dma((6,)),
         ]
-        + [dma(ring)] * 8
-        + [dma((1,)), dma((4, SIDE - 1)), dma((4, PUMPS - SIDE)), dma((1,))],
+        + gather_sems
+        + [dma(ring)] * 4
+        + gather_sems,
         compiler_params=pltpu.CompilerParams(
             collective_id=0, has_side_effects=True, vmem_limit_bytes=60 * 1024 * 1024
         ),

time: 98.7 us -> 98.4 us (level)
  no operation moved by 1% of the time
where the time goes in v4:
time: 98.4 us; the launch traced here: 98.2 us
  Pallas kernels  97.5 us (99%)
    pallas_call x1, Pallas kernels, run_layer(): pl.pallas_call(layer_kernel, out_shape=(jax.ShapeDtypeStruct((rows, width...  89.5 us
    pallas_call x1, Pallas kernels, fill_pages(): pl.pallas_call(fill_kernel, out_shape=(jax.ShapeDtypeStruct((requests * m...  7.98 us

profile of v4, /device:TPU:0, one launch (start us, length us, event | category | flops | bytes accessed | tf_op | source)
XLA Modules:
  0.0 98.2 jit_solution(4882735330276232354)
XLA Ops:
  0.6 89.5 %layer.1 = (bf16[128,2048]{1,0:T(8,128)(2,1)}, bf16[16384,2,256]{2,1,0:T(2,128)(2,1)}, s32[32,128]{1,0:T(8,128)}) custom-call(bf16[128,2048]{1,0:T(8,128)(2,1)} %hidden.1, s32[32,512]{1,0:T(8,128)} %seg.1, bf16[2048]{0:T(1024)(128)(2,1)} %ln_attn.1, bf16[2048,512]{1,0:T(8,128)(2,1)} %w_query.1, bf16[2048,256]{1,0:T(8,128)(2,1)} %w_key.1, ...), custom_call_target="tpu_custom_call" | custom-call | tf_op jit(solution)/shard_map/layer/pallas_call | solution.py:627
  90.2 8.0 %fill_pages.1 = (bf16[512,16,2,256]{3,2,1,0:T(2,128)(2,1)}, bf16[128,2048]{1,0:T(8,128)(2,1)}) custom-call(s32[16,32]{1,0:T(8,128)} %bitcast.1, s32[32]{0:T(128)} %prompt_hbm.1, s32[32,128]{1,0:T(8,128)} %get-tuple-element.7.bounds_hbm, bf16[128,2048]{1,0:T(8,128)(2,1)} %get-tuple-element.8.layer_hbm, bf16[16384,2,256]{2,1,0:T(2,128)(2,1)} %get-tuple-element.9.rows_ref), custom_call_target="tpu_custom_call" | custom-call | tf_op jit(solution)/shard_map/fill_pages/pallas_call | solution.py:116

commit v5 on v4

--- a/solution.py
+++ b/solution.py
@@ -140,7 +140,6 @@
 HALF = 64
 SUBS = 2
 SIDE = 4
-UNIT = 128
 PUMPS = SIDE * SIDE
 
 
@@ -202,10 +201,14 @@
     ag2_recv,
     rs2_send,
     rs2_recv,
-    kv_send,
-    kv1_recv,
-    kv2_recv,
-    kv_pair_recv,
+    kv_send_a,
+    kv1_recv_a,
+    kv2_recv_a,
+    kv_pair_recv_a,
+    kv_send_b,
+    kv1_recv_b,
+    kv2_recv_b,
+    kv_pair_recv_b,
 ):
     x = lax.axis_index("mp")
     c = lax.axis_index("req")
@@ -312,7 +315,8 @@
     flows = ((0, 0), (0, 1), (1, 0), (1, 1))
 
     def make_pump(block_of, send, recv1, recv2, pair_recv):
-        def pump(p):
+        def pump(p, own=None):
+            p = jnp.int32(p)
             b, k = lax.rem(p, SIDE), p // SIDE
             for f, (axis, d) in enumerate(flows):
                 step = 1 if d == 0 else -1
@@ -322,6 +326,7 @@
                     block = block_of(f, turn(y - step * b), turn(z - step * k))
                 else:
                     block = block_of(f, turn(y - step * k), turn(z - step * b))
+                source = block if own is None else own(f)
 
                 @pl.when((p >= 1) & (p < SIDE))
                 def _():
@@ -333,26 +338,37 @@
 
                 @pl.when(p < SIDE - 1)
                 def _():
-                    remote(block, block, send.at[0], recv1.at[f, p], first).start()
+                    remote(source, block, send.at[0], recv1.at[f, p], first).start()
 
                 @pl.when(p < PUMPS - SIDE)
                 def _():
-                    remote(block, block, send.at[1], recv2.at[f, p], second).start()
-
-                remote(block, block, send.at[2], pair_recv.at[0], pair).start()
+                    remote(source, block, send.at[1], recv2.at[f, p], second).start()
+
+                remote(source, block, send.at[2], pair_recv.at[0], pair).start()
 
         return pump
 
     seq = SIDE * rows
     strip = width // len(flows)
 
-    def kv_block(f, oy, oz):
-        return kv.at[pl.ds(pl.multiple_of(req_of(oy, oz, core) * seq + f * UNIT, UNIT), UNIT)]
+    def piece_at(j, d):
+        chunk = turn(x - j) if d == 0 else turn(x + j)
+        return pl.multiple_of(chunk * rows + d * HALF, HALF)
+
+    def kv_block(stage):
+        def block_of(f, oy, oz):
+            return kv.at[pl.ds(req_of(oy, oz, core) * seq + piece_at(2 * stage + f // 2, f % 2), HALF)]
+
+        return block_of
+
+    def kv_source(stage):
+        return lambda f: kvbuf.at[pl.ds(piece_at(2 * stage + f // 2, f % 2), HALF)]
 
     def w_block(f, oy, oz):
         return wfull.at[:, oy, oz, core, :, pl.ds(f * strip, strip)]
 
-    pump = make_pump(kv_block, kv_send, kv1_recv, kv2_recv, kv_pair_recv)
+    pump_a = make_pump(kv_block(0), kv_send_a, kv1_recv_a, kv2_recv_a, kv_pair_recv_a)
+    pump_b = make_pump(kv_block(1), kv_send_b, kv1_recv_b, kv2_recv_b, kv_pair_recv_b)
     w_pump = make_pump(w_block, w_send, w1_recv, w2_recv, w_pair_recv)
 
     def settle(send, pair_recv, first, second, last):
@@ -370,6 +386,10 @@
             for p in range(SUBS):
                 gather_advance(hbuf, ag1_send, ag1_recv, j, p)
                 w_pump(3 * j - 2 + p)
+
+                @pl.when(j > 1)
+                def _():
+                    pump_a(3 * j - 5 + p)
 
         a, b = turn(x - j), turn(x + j)
         normed = rms(ring_rows(hbuf, j), gain_attn).astype(jnp.bfloat16)
@@ -408,13 +428,21 @@
 
         w_pump(3 * j)
 
+        @pl.when(j == 1)
+        def _():
+            pump_a(0, kv_source(0))
+
+        @pl.when(j > 1)
+        def _():
+            pump_a(3 * j - 3)
+
     kv_own = pltpu.make_async_copy(kvbuf, kv.at[pl.ds(c * seq, seq)], local_sem.at[2 * SUBS + len(weights)])
     kv_own.start()
 
-    w_pump(jnp.int32(3 * SIDE - 2))
-    w_pump(jnp.int32(3 * SIDE - 1))
-    kv_own.wait()
-    pump(jnp.int32(0))
+    w_pump(3 * SIDE - 2)
+    pump_b(0, kv_source(1))
+    w_pump(3 * SIDE - 1)
+    pump_a(7)
 
     def a_copy(n, src, dst, near):
         return remote(src, dst, a_send.at[n], a_recv.at[n], near)
@@ -472,7 +500,9 @@
             head_copy(2, i).start()
             head_copy(3, i).start()
 
-        w_pump(jnp.int32(3 * SIDE + i))
+        w_pump(3 * SIDE + i)
+        if i % 2 == 1:
+            pump_a(8 + i // 2)
     piece = width // SUBS
 
     def sum_step(send_buf, recv_buf, send, recv, j, d, n):
@@ -510,12 +540,15 @@
         before = [hbuf[x, d, :, :, columns].reshape(HALF, piece) for d in range(2)]
         send2f[n] = jnp.concatenate(before, axis=0).astype(jnp.float32)
         add_heads(mixed, wo[:, columns], n)
+    pump_b(1)
+    pump_a(10)
     half = wfull.at[:, :, :, 0]
     remote(half, half, w_send.at[2], w_pair_recv.at[0], pair).wait_recv()
     head_copy(1).wait_recv()
     add_source(1)
     head_copy(0).wait_recv()
     add_source(3)
+    pump_a(11)
     for move in relays:
         move.wait_recv()
     add_source(2)
@@ -526,7 +559,8 @@
     for p in range(SUBS):
         for d in range(2):
             gather_step(abuf, ag2_send, ag2_recv, 0, d, p).start()
-    pump(jnp.int32(1))
+    pump_b(2)
+    pump_a(12)
 
     for move in moves[2 * SUBS + 4 :]:
         move.wait()
@@ -546,13 +580,17 @@
         def _():
             for p in range(SUBS):
                 gather_advance(abuf, ag2_send, ag2_recv, j, p)
-                pump(4 * j - 1 + p)
+                pump_b(4 * j + p)
+
+                @pl.when(j == 1)
+                def _():
+                    pump_a(14 + p)
 
         actbuf[...] = activation(j)
 
         @pl.when(j > 0)
         def _():
-            pump(4 * j + 1)
+            pump_b(4 * j + 2)
 
         @pl.when(j > 0)
         def _():
@@ -570,11 +608,11 @@
         @pl.when(j == 0)
         def _():
             ownbuf[...] = actbuf[...]
-
-        pump(4 * j + 2)
+            pump_a(13)
+
+        pump_b(4 * j + 3)
 
     act = ownbuf[...]
-    pump(jnp.int32(PUMPS - 1))
     for n in range(SUBS):
         part = add_arrived(down_part(act, n), *ring2, SIDE - 2, n)
         for d in range(2):
@@ -599,15 +637,12 @@
     settle(
         w_send, w_pair_recv, wfull.at[:, 0, pl.ds(0, SIDE - 1), 0], wfull.at[:, pl.ds(0, SIDE - 1), :, 0], half
     )
-    settle(
-        kv_send,
-        kv_pair_recv,
-        kv.at[pl.ds(0, UNIT * len(flows) * (SIDE - 1))],
-        kv.at[pl.ds(0, UNIT * len(flows) * (PUMPS - SIDE))],
-        kv.at[pl.ds(0, UNIT * len(flows) * PUMPS)],
-    )
-    got = kv.at[pl.ds(0, UNIT * len(flows) * PUMPS)]
-    remote(got, got, kv_send.at[2], kv_pair_recv.at[0], pair).wait_recv()
+    kv_own.wait()
+    units = HALF * len(flows)
+    got = kv.at[pl.ds(0, units * PUMPS)]
+    for send, pair_recv in ((kv_send_a, kv_pair_recv_a), (kv_send_b, kv_pair_recv_b)):
+        settle(send, pair_recv, kv.at[pl.ds(0, units * (SIDE - 1))], kv.at[pl.ds(0, units * (PUMPS - SIDE))], got)
+        remote(got, got, send.at[2], pair_recv.at[0], pair).wait_recv()
 
 
 def run_layer(hidden, seg, ln_attn, w_query, w_key, w_value, q_gain, k_gain, w_out, ln_mlp, w_gate, w_up, w_down):
@@ -666,7 +701,7 @@
         ]
         + gather_sems
         + [dma(ring)] * 4
-        + gather_sems,
+        + gather_sems * 2,
         compiler_params=pltpu.CompilerParams(
             collective_id=0, has_side_effects=True, vmem_limit_bytes=60 * 1024 * 1024
         ),

time: 98.4 us -> 111 us (1.13)
  Pallas kernels: 97.5 us -> 110 us
    pallas_call x1, Pallas kernels: 89.5 us -> 102 us  [run_layer(): pl.pallas_call(layer_kernel, out_shape=(jax.ShapeDtypeStruct((rows, width...]
where the time goes in v5:
time: 111 us; the launch traced here: 110 us
  Pallas kernels  110 us (99%)
    pallas_call x1, Pallas kernels, run_layer(): pl.pallas_call(layer_kernel, out_shape=(jax.ShapeDtypeStruct((rows, width...  102 us
    pallas_call x1, Pallas kernels, fill_pages(): pl.pallas_call(fill_kernel, out_shape=(jax.ShapeDtypeStruct((requests * m...  7.91 us

profile of v5, /device:TPU:0, one launch (start us, length us, event | category | flops | bytes accessed | tf_op | source)
XLA Modules:
  0.0 110.4 jit_solution(7099145199237907017)
XLA Ops:
  0.6 101.8 %layer.1 = (bf16[128,2048]{1,0:T(8,128)(2,1)}, bf16[16384,2,256]{2,1,0:T(2,128)(2,1)}, s32[32,128]{1,0:T(8,128)}) custom-call(bf16[128,2048]{1,0:T(8,128)(2,1)} %hidden.1, s32[32,512]{1,0:T(8,128)} %seg.1, bf16[2048]{0:T(1024)(128)(2,1)} %ln_attn.1, bf16[2048,512]{1,0:T(8,128)(2,1)} %w_query.1, bf16[2048,256]{1,0:T(8,128)(2,1)} %w_key.1, ...), custom_call_target="tpu_custom_call" | custom-call | tf_op jit(solution)/shard_map/layer/pallas_call | solution.py:662
  102.4 7.9 %fill_pages.1 = (bf16[512,16,2,256]{3,2,1,0:T(2,128)(2,1)}, bf16[128,2048]{1,0:T(8,128)(2,1)}) custom-call(s32[16,32]{1,0:T(8,128)} %bitcast.1, s32[32]{0:T(128)} %prompt_hbm.1, s32[32,128]{1,0:T(8,128)} %get-tuple-element.7.bounds_hbm, bf16[128,2048]{1,0:T(8,128)(2,1)} %get-tuple-element.8.layer_hbm, bf16[16384,2,256]{2,1,0:T(2,128)(2,1)} %get-tuple-element.9.rows_ref), custom_call_target="tpu_custom_call" | custom-call | tf_op jit(solution)/shard_map/fill_pages/pallas_call | solution.py:116

commit v6 on v5

--- a/solution.py
+++ b/solution.py
@@ -16,17 +16,11 @@
 THETA = 1000000.0
 
 
-SLOTS = 16
-AHEAD = 12
-
-
 def fill_kernel(
-    table_hbm, prompt_hbm, bounds_hbm, layer_hbm, rows_ref, out_ref, layer_out, table, prompt, bounds, held, slots,
-    zeros, small_sem, in_sem, out_sem,
+    table_hbm, prompt_hbm, bounds_hbm, layer_hbm, rows_ref, out_ref, layer_out, table, prompt, bounds, held, edges,
+    zeros, small_sem, out_sem,
 ):
     most, requests = table.shape
-    span = most * PAGE
-    last = rows_ref.shape[0] - span
     seq = rows_ref.shape[0] // bounds.shape[0]
     smalls = [
         pltpu.make_async_copy(src, dst, small_sem.at[n])
@@ -42,70 +36,42 @@
         small.wait()
     layer_copy.start()
 
-    def place(r):
+    @pl.loop(0, requests)
+    def _(r):
         p = prompt[r]
         g = p // PROMPTS_DEV
         s = p - g * PROMPTS_DEV
         low = jnp.where(s == 0, 0, jnp.where(s == 1, bounds[g, 0], bounds[g, 1]))
         high = jnp.where(s == 0, bounds[g, 0], jnp.where(s == 1, bounds[g, 1], seq))
-        begin = g * seq + low
-        return begin, high - low, jnp.minimum(begin, last)
-
-    def fetch(r, slot):
-        at = place(r)[2]
-        return pltpu.make_async_copy(
-            rows_ref.at[pl.ds(at, span)], slots.at[slot, pl.ds(0, span)], in_sem.at[slot]
-        )
-
-    def drain(slot):
-        pltpu.make_async_copy(
-            out_ref.at[pl.ds(0, most)], out_ref.at[pl.ds(0, most)], out_sem.at[slot]
-        ).wait()
-
-    for r in range(min(AHEAD, requests)):
-        fetch(r, r).start()
-
-    @pl.loop(0, requests)
-    def _(r):
-        slot = lax.rem(r, SLOTS)
-        fetch(r, slot).wait()
-        begin, length, at = place(r)
-        shift = begin - at
+        begin, length = g * seq + low, high - low
         full = length // PAGE
         rest = length - full * PAGE
 
         @pl.when(rest > 0)
         def _():
-            edge = shift + full * PAGE
-            tail = slots[slot, pl.ds(edge, PAGE)]
-            row = lax.broadcasted_iota(jnp.int32, tail.shape, 0)
-            slots[slot, pl.ds(edge, PAGE)] = jnp.where(row < rest, tail, jnp.zeros_like(tail))
+            at = begin + full * PAGE
+            for o in range(PAGE):
+                line = rows_ref[pl.ds(jnp.minimum(at + o, rows_ref.shape[0] - 1), 1)]
+                edges[r, pl.ds(o, 1)] = jnp.where(o < rest, line, jnp.zeros_like(line))
 
         for e in range(most):
             page = table[e, r]
 
-            @pl.when(e * PAGE < length)
+            @pl.when(e < full)
             def _():
                 pltpu.make_async_copy(
-                    slots.at[slot, pl.ds(shift + e * PAGE, PAGE)], out_ref.at[page], out_sem.at[slot]
+                    rows_ref.at[pl.ds(begin + e * PAGE, PAGE)], out_ref.at[page], out_sem.at[0]
                 ).start()
 
             @pl.when(e * PAGE >= length)
             def _():
-                pltpu.make_async_copy(zeros, out_ref.at[page], out_sem.at[slot]).start()
-
-        @pl.when(r + AHEAD < requests)
-        def _():
-            other = lax.rem(r + AHEAD, SLOTS)
-
-            @pl.when(r + AHEAD >= SLOTS)
-            def _():
-                drain(other)
-
-            fetch(r + AHEAD, other).start()
-
-    for r in range(max(0, requests - SLOTS), requests):
-        drain(r % SLOTS)
+                pltpu.make_async_copy(zeros, out_ref.at[page], out_sem.at[0]).start()
+
+        @pl.when(rest > 0)
+        def _():
+            pltpu.make_async_copy(edges.at[r], out_ref.at[table[full, r]], out_sem.at[0]).start()
+
+    pltpu.make_async_copy(out_ref, out_ref, out_sem.at[0]).wait()
     layer_copy.wait()
 
 
@@ -119,19 +85,19 @@
             jax.ShapeDtypeStruct((requests * most, PAGE) + unit, rows.dtype),
             jax.ShapeDtypeStruct(layer.shape, layer.dtype),
         ),
-        in_specs=[hbm] * 5,
+        in_specs=[hbm] * 4 + [pl.BlockSpec(memory_space=pltpu.VMEM)],
         out_specs=(hbm, hbm),
         scratch_shapes=[
             pltpu.SMEM((most, requests), jnp.int32),
             pltpu.SMEM((requests,), jnp.int32),
             pltpu.SMEM(bounds.shape, jnp.int32),
             pltpu.VMEM(layer.shape, layer.dtype),
-            pltpu.VMEM((SLOTS, (most + 1) * PAGE) + unit, rows.dtype),
+            pltpu.VMEM((requests, PAGE) + unit, rows.dtype),
             pltpu.VMEM((PAGE,) + unit, rows.dtype),
             pltpu.SemaphoreType.DMA((5,)),
-            pltpu.SemaphoreType.DMA((SLOTS,)),
-            pltpu.SemaphoreType.DMA((SLOTS,)),
+            pltpu.SemaphoreType.DMA((1,)),
         ],
+        compiler_params=pltpu.CompilerParams(vmem_limit_bytes=46 * 1024 * 1024),
         name="fill_pages",
     )(page_table.T, request_prompt, bounds, layer, rows)
 
@@ -385,11 +351,15 @@
         def _():
             for p in range(SUBS):
                 gather_advance(hbuf, ag1_send, ag1_recv, j, p)
-                w_pump(3 * j - 2 + p)
+
+                @pl.when(j == 1)
+                def _():
+                    w_pump(1 + p)
 
                 @pl.when(j > 1)
                 def _():
-                    pump_a(3 * j - 5 + p)
+                    w_pump(5 * j - 6 + 2 * p)
+                    w_pump(5 * j - 5 + 2 * p)
 
         a, b = turn(x - j), turn(x + j)
         normed = rms(ring_rows(hbuf, j), gain_attn).astype(jnp.bfloat16)
@@ -426,23 +396,18 @@
             for k in (1, 3, 2):
                 out_exchange(k).wait_recv()
 
-        w_pump(3 * j)
-
-        @pl.when(j == 1)
+        w_pump(jnp.maximum(5 * j - 2, 0))
+
+        @pl.when(j == 2)
         def _():
             pump_a(0, kv_source(0))
-
-        @pl.when(j > 1)
-        def _():
-            pump_a(3 * j - 3)
 
     kv_own = pltpu.make_async_copy(kvbuf, kv.at[pl.ds(c * seq, seq)], local_sem.at[2 * SUBS + len(weights)])
     kv_own.start()
 
-    w_pump(3 * SIDE - 2)
+    pump_a(1)
     pump_b(0, kv_source(1))
-    w_pump(3 * SIDE - 1)
-    pump_a(7)
+    w_pump(14)
 
     def a_copy(n, src, dst, near):
         return remote(src, dst, a_send.at[n], a_recv.at[n], near)
@@ -500,9 +465,8 @@
             head_copy(2, i).start()
             head_copy(3, i).start()
 
-        w_pump(3 * SIDE + i)
-        if i % 2 == 1:
-            pump_a(8 + i // 2)
+        if i == 2:
+            w_pump(15)
     piece = width // SUBS
 
     def sum_step(send_buf, recv_buf, send, recv, j, d, n):
@@ -534,6 +498,7 @@
     for n, move in enumerate(relays):
         head_copy(2 + n).wait_recv()
         move.start()
+    pump_a(2)
     mixed = attbuf[x].reshape(rows, heads * HD)
     for n in range(SUBS):
         columns = slice(n * piece, (n + 1) * piece)
@@ -541,14 +506,12 @@
         send2f[n] = jnp.concatenate(before, axis=0).astype(jnp.float32)
         add_heads(mixed, wo[:, columns], n)
     pump_b(1)
-    pump_a(10)
     half = wfull.at[:, :, :, 0]
     remote(half, half, w_send.at[2], w_pair_recv.at[0], pair).wait_recv()
     head_copy(1).wait_recv()
     add_source(1)
     head_copy(0).wait_recv()
     add_source(3)
-    pump_a(11)
     for move in relays:
         move.wait_recv()
     add_source(2)
@@ -559,8 +522,8 @@
     for p in range(SUBS):
         for d in range(2):
             gather_step(abuf, ag2_send, ag2_recv, 0, d, p).start()
-    pump_b(2)
-    pump_a(12)
+    for p in range(3, 7):
+        pump_a(p)
 
     for move in moves[2 * SUBS + 4 :]:
         move.wait()
@@ -580,17 +543,43 @@
         def _():
             for p in range(SUBS):
                 gather_advance(abuf, ag2_send, ag2_recv, j, p)
-                pump_b(4 * j + p)
-
-                @pl.when(j == 1)
+
+                @pl.when(j > 1)
                 def _():
-                    pump_a(14 + p)
+                    pump_b(4 * j - 2 + p)
+
+                if p == 0:
+
+                    @pl.when(j == 1)
+                    def _():
+                        pump_a(7)
+
+                    pump_a(4 * j + 3 + lax.select(j == 1, 1, 0))
+                else:
+
+                    @pl.when(j == 2)
+                    def _():
+                        pump_a(12)
 
         actbuf[...] = activation(j)
 
-        @pl.when(j > 0)
-        def _():
-            pump_b(4 * j + 2)
+        @pl.when(j == 0)
+        def _():
+            pump_b(2)
+
+        @pl.when(j == 1)
+        def _():
+            pump_b(3)
+            pump_b(4)
+            pump_b(5)
+
+        @pl.when(j == 2)
+        def _():
+            pump_a(13)
+
+        @pl.when(j > 1)
+        def _():
+            pump_b(4 * j)
 
         @pl.when(j > 0)
         def _():
@@ -608,11 +597,23 @@
         @pl.when(j == 0)
         def _():
             ownbuf[...] = actbuf[...]
-            pump_a(13)
-
-        pump_b(4 * j + 3)
+
+        @pl.when(j == 1)
+        def _():
+            pump_a(9)
+            pump_a(10)
+
+        @pl.when(j == 2)
+        def _():
+            pump_a(14)
+
+        @pl.when(j > 1)
+        def _():
+            pump_b(4 * j + 1)
 
     act = ownbuf[...]
+    pump_b(14)
+    pump_b(15)
     for n in range(SUBS):
         part = add_arrived(down_part(act, n), *ring2, SIDE - 2, n)
         for d in range(2):
@@ -663,11 +664,11 @@
         layer_kernel,
         out_shape=(
             jax.ShapeDtypeStruct((rows, width), bf16),
-            jax.ShapeDtypeStruct((seg.shape[0] * seq, kvw // HD, 2 * HD), bf16),
+            pltpu.VMEM((seg.shape[0] * seq, kvw // HD, 2 * HD), bf16),
             jax.ShapeDtypeStruct((seg.shape[0], HD), jnp.int32),
         ),
         in_specs=[hbm, vmem, vmem, hbm, hbm, hbm, vmem, vmem, hbm, vmem, hbm, hbm, hbm],
-        out_specs=(vmem, hbm, vmem),
+        out_specs=(vmem, vmem, vmem),
         scratch_shapes=[
             pltpu.VMEM((SIDE, 2, SUBS, sub, width), bf16),
             pltpu.VMEM((SIDE, 2, SUBS, sub, width), bf16),
@@ -703,7 +704,7 @@
         + [dma(ring)] * 4
         + gather_sems * 2,
         compiler_params=pltpu.CompilerParams(
-            collective_id=0, has_side_effects=True, vmem_limit_bytes=60 * 1024 * 1024
+            collective_id=0, has_side_effects=True, vmem_limit_bytes=46 * 1024 * 1024
         ),
         name="layer",
     )(hidden, seg, ln_attn, w_query, w_key, w_value, q_gain, k_gain, w_out, ln_mlp, w_gate, w_up, w_down)
@@ -741,6 +742,7 @@
         w_up,
         w_down,
     )
+    everything = pltpu.with_memory_space_constraint(everything, pltpu.VMEM)
     cache, result = fill_pages(page_table, request_prompt, bounds, result, everything)
     return (result, cache)
 

time: 111 us -> 94.3 us (0.85)
  Pallas kernels: 110 us -> 93.5 us
    pallas_call x1, Pallas kernels: 102 us -> 88 us  [run_layer(): pl.pallas_call(layer_kernel, out_shape=(jax.ShapeDtypeStruct((rows, width...]
    pallas_call x1, Pallas kernels: 7.91 us -> 5.51 us  [fill_pages(): pl.pallas_call(fill_kernel, out_shape=(jax.ShapeDtypeStruct((requests * m...]
where the time goes in v6:
time: 94.3 us; the launch traced here: 94.1 us
  Pallas kernels  93.5 us (99%)
    pallas_call x1, Pallas kernels, run_layer(): pl.pallas_call(layer_kernel, out_shape=(jax.ShapeDtypeStruct((rows, width...  88 us
    pallas_call x1, Pallas kernels, fill_pages(): pl.pallas_call(fill_kernel, out_shape=(jax.ShapeDtypeStruct((requests * m...  5.51 us

profile of v6, /device:TPU:0, one launch (start us, length us, event | category | flops | bytes accessed | tf_op | source)
XLA Modules:
  0.0 94.1 jit_solution(17120405249639800127)
XLA Ops:
  0.6 88.0 %layer.1 = (bf16[128,2048]{1,0:T(8,128)(2,1)}, bf16[16384,2,256]{2,1,0:T(2,128)(2,1)S(1)}, s32[32,128]{1,0:T(8,128)}) custom-call(bf16[128,2048]{1,0:T(8,128)(2,1)} %hidden.1, s32[32,512]{1,0:T(8,128)} %seg.1, bf16[2048]{0:T(1024)(128)(2,1)} %ln_attn.1, bf16[2048,512]{1,0:T(8,128)(2,1)} %w_query.1, bf16[2048,256]{1,0:T(8,128)(2,1)} %w_key.1, ...), custom_call_target="tpu_custom_call" | custom-call | tf_op jit(solution)/shard_map/layer/pallas_call | solution.py:663
  88.6 5.5 %fill_pages.1 = (bf16[512,16,2,256]{3,2,1,0:T(2,128)(2,1)}, bf16[128,2048]{1,0:T(8,128)(2,1)}) custom-call(s32[16,32]{1,0:T(8,128)} %bitcast.1, s32[32]{0:T(128)} %prompt_hbm.1, s32[32,128]{1,0:T(8,128)} %get-tuple-element.7.bounds_hbm, bf16[128,2048]{1,0:T(8,128)(2,1)} %get-tuple-element.8.layer_hbm, bf16[16384,2,256]{2,1,0:T(2,128)(2,1)S(1)} %get-tuple-element.9.rows_ref), custom_call_target="tpu_custom_call" | custom-call | tf_op jit(solution)/shard_map/fill_pages/pallas_call | solution.py:82

commit v7 on v6

--- a/solution.py
+++ b/solution.py
@@ -17,18 +17,18 @@
 
 
 def fill_kernel(
-    table_hbm, prompt_hbm, bounds_hbm, layer_hbm, rows_ref, out_ref, layer_out, table, prompt, bounds, held, edges,
-    zeros, small_sem, out_sem,
+    table_hbm, prompt_hbm, bounds_ref, layer_ref, rows_ref, out_ref, layer_out, table, prompt, bounds, edges, zeros,
+    small_sem, out_sem,
 ):
     most, requests = table.shape
     seq = rows_ref.shape[0] // bounds.shape[0]
     smalls = [
         pltpu.make_async_copy(src, dst, small_sem.at[n])
         for n, (src, dst) in enumerate(
-            ((table_hbm, table), (prompt_hbm, prompt), (bounds_hbm, bounds), (layer_hbm, held))
+            ((table_hbm, table), (prompt_hbm, prompt), (bounds_ref, bounds))
         )
     ]
-    layer_copy = pltpu.make_async_copy(held, layer_out, small_sem.at[4])
+    layer_copy = pltpu.make_async_copy(layer_ref, layer_out, small_sem.at[3])
     for small in smalls:
         small.start()
     zeros[...] = jnp.zeros_like(zeros)
@@ -85,16 +85,15 @@
             jax.ShapeDtypeStruct((requests * most, PAGE) + unit, rows.dtype),
             jax.ShapeDtypeStruct(layer.shape, layer.dtype),
         ),
-        in_specs=[hbm] * 4 + [pl.BlockSpec(memory_space=pltpu.VMEM)],
+        in_specs=[hbm] * 2 + [pl.BlockSpec(memory_space=pltpu.VMEM)] * 3,
         out_specs=(hbm, hbm),
         scratch_shapes=[
             pltpu.SMEM((most, requests), jnp.int32),
             pltpu.SMEM((requests,), jnp.int32),
             pltpu.SMEM(bounds.shape, jnp.int32),
-            pltpu.VMEM(layer.shape, layer.dtype),
             pltpu.VMEM((requests, PAGE) + unit, rows.dtype),
             pltpu.VMEM((PAGE,) + unit, rows.dtype),
-            pltpu.SemaphoreType.DMA((5,)),
+            pltpu.SemaphoreType.DMA((4,)),
             pltpu.SemaphoreType.DMA((1,)),
         ],
         compiler_params=pltpu.CompilerParams(vmem_limit_bytes=46 * 1024 * 1024),
@@ -115,21 +114,26 @@
 
 def layer_kernel(
     hidden,
-    seg,
-    ln_attn,
+    seg_hbm,
+    ln_attn_hbm,
     w_query,
     w_key,
     w_value,
-    q_gain,
-    k_gain,
+    q_gain_hbm,
+    k_gain_hbm,
     w_out,
-    ln_mlp,
+    ln_mlp_hbm,
     w_gate,
     w_up,
     w_down,
     out,
     kv,
     bounds,
+    seg,
+    ln_attn,
+    q_gain,
+    k_gain,
+    ln_mlp,
     hbuf,
     abuf,
     wq,
@@ -207,7 +211,13 @@
             )
     for n, (src, dst) in enumerate(weights):
         moves.append(pltpu.make_async_copy(src, dst, local_sem.at[2 * SUBS + n]))
-    for move in moves:
+    smalls = [
+        pltpu.make_async_copy(src, dst, local_sem.at[2 * SUBS + len(weights) + 1 + n])
+        for n, (src, dst) in enumerate(
+            ((seg_hbm, seg), (ln_attn_hbm, ln_attn), (q_gain_hbm, q_gain), (k_gain_hbm, k_gain), (ln_mlp_hbm, ln_mlp))
+        )
+    ]
+    for move in smalls + moves:
         move.start()
 
     barrier = pltpu.get_barrier_semaphore()
@@ -256,6 +266,9 @@
         for d in range(2):
             own = hidden.at[pl.ds(d * HALF + p * sub, sub)]
             remote(own, hbuf.at[x, d, p], ag1_send.at[0, d, p], ag1_recv.at[0, d, p], x_near[d]).start()
+
+    for move in smalls:
+        move.wait()
 
     def below(table, bound):
         return jnp.sum((table < bound).astype(jnp.int32), axis=1, keepdims=True)
@@ -345,6 +358,10 @@
     for move in moves[: 2 * SUBS + 3]:
         move.wait()
 
+    for k in (1, 3, 2):
+        out_exchange(k).wait_recv()
+    w_pump(0)
+
     @pl.loop(0, SIDE)
     def _(j):
         @pl.when(j > 0)
@@ -356,10 +373,16 @@
                 def _():
                     w_pump(1 + p)
 
-                @pl.when(j > 1)
+                @pl.when(j == 2)
                 def _():
-                    w_pump(5 * j - 6 + 2 * p)
-                    w_pump(5 * j - 5 + 2 * p)
+                    w_pump(4 + 2 * p)
+                    w_pump(5 + 2 * p)
+                    if p == 1:
+                        w_pump(8)
+
+                @pl.when(j == 3)
+                def _():
+                    w_pump(10 + p)
 
         a, b = turn(x - j), turn(x + j)
         normed = rms(ring_rows(hbuf, j), gain_attn).astype(jnp.bfloat16)
@@ -391,12 +414,9 @@
         vbuf[a, 0] = value[:HALF]
         vbuf[b, 1] = value[HALF:]
 
-        @pl.when(j == 0)
-        def _():
-            for k in (1, 3, 2):
-                out_exchange(k).wait_recv()
-
-        w_pump(jnp.maximum(5 * j - 2, 0))
+        @pl.when(j > 0)
+        def _():
+            w_pump(lax.select(j == 1, 3, 3 * j + 3))
 
         @pl.when(j == 2)
         def _():
@@ -407,7 +427,7 @@
 
     pump_a(1)
     pump_b(0, kv_source(1))
-    w_pump(14)
+    w_pump(13)
 
     def a_copy(n, src, dst, near):
         return remote(src, dst, a_send.at[n], a_recv.at[n], near)
@@ -465,8 +485,8 @@
             head_copy(2, i).start()
             head_copy(3, i).start()
 
-        if i == 2:
-            w_pump(15)
+        if i < 2:
+            w_pump(14 + i)
     piece = width // SUBS
 
     def sum_step(send_buf, recv_buf, send, recv, j, d, n):
@@ -663,13 +683,18 @@
     return pl.pallas_call(
         layer_kernel,
         out_shape=(
-            jax.ShapeDtypeStruct((rows, width), bf16),
+            pltpu.VMEM((rows, width), bf16),
             pltpu.VMEM((seg.shape[0] * seq, kvw // HD, 2 * HD), bf16),
-            jax.ShapeDtypeStruct((seg.shape[0], HD), jnp.int32),
+            pltpu.VMEM((seg.shape[0], HD), jnp.int32),
         ),
-        in_specs=[hbm, vmem, vmem, hbm, hbm, hbm, vmem, vmem, hbm, vmem, hbm, hbm, hbm],
+        in_specs=[hbm] * 13,
         out_specs=(vmem, vmem, vmem),
         scratch_shapes=[
+            pltpu.VMEM(seg.shape, seg.dtype),
+            pltpu.VMEM(ln_attn.shape, bf16),
+            pltpu.VMEM(q_gain.shape, bf16),
+            pltpu.VMEM(k_gain.shape, bf16),
+            pltpu.VMEM(ln_mlp.shape, bf16),
             pltpu.VMEM((SIDE, 2, SUBS, sub, width), bf16),
             pltpu.VMEM((SIDE, 2, SUBS, sub, width), bf16),
             pltpu.VMEM(w_query.shape, bf16),
@@ -692,7 +717,7 @@
             pltpu.VMEM((2, HALF, heads_w), bf16),
             blocks,
             blocks,
-            dma((2 * SUBS + 8,)),
+            dma((2 * SUBS + 13,)),
             dma(ring),
             dma(ring),
             dma((SIDE - 1,)),
@@ -742,7 +767,9 @@
         w_up,
         w_down,
     )
-    everything = pltpu.with_memory_space_constraint(everything, pltpu.VMEM)
+    result, everything, bounds = (
+        pltpu.with_memory_space_constraint(array, pltpu.VMEM) for array in (result, everything, bounds)
+    )
     cache, result = fill_pages(page_table, request_prompt, bounds, result, everything)
     return (result, cache)
 

time: 94.3 us -> 91.8 us (0.973)
  Pallas kernels: 93.5 us -> 91 us
    pallas_call x1, Pallas kernels: 88 us -> 85.7 us  [run_layer(): pl.pallas_call(layer_kernel, out_shape=(pltpu.VMEM((rows, width), bf16),...]
where the time goes in v7:
time: 91.8 us; the launch traced here: 91.6 us
  Pallas kernels  91 us (99%)
    pallas_call x1, Pallas kernels, run_layer(): pl.pallas_call(layer_kernel, out_shape=(pltpu.VMEM((rows, width), bf16),...  85.7 us
    pallas_call x1, Pallas kernels, fill_pages(): pl.pallas_call(fill_kernel, out_shape=(jax.ShapeDtypeStruct((requests * m...  5.3 us

profile of v7, /device:TPU:0, one launch (start us, length us, event | category | flops | bytes accessed | tf_op | source)
XLA Modules:
  0.0 91.6 jit_solution(6894458226374882687)
XLA Ops:
  0.6 85.7 %layer.1 = (bf16[128,2048]{1,0:T(8,128)(2,1)S(1)}, bf16[16384,2,256]{2,1,0:T(2,128)(2,1)S(1)}, s32[32,128]{1,0:T(8,128)S(1)}) custom-call(bf16[128,2048]{1,0:T(8,128)(2,1)} %hidden.1, s32[32,512]{1,0:T(8,128)} %seg_hbm.1, bf16[2048]{0:T(1024)(128)(2,1)} %ln_attn_hbm.1, bf16[2048,512]{1,0:T(8,128)(2,1)} %w_query.1, bf16[2048,256]{1,0:T(8,128)(2,1)} %w_key.1, ...), custom_call_target="tpu_custom_call" | custom-call | tf_op jit(solution)/shard_map/layer/pallas_call | solution.py:683
  86.3 5.3 %fill_pages.1 = (bf16[512,16,2,256]{3,2,1,0:T(2,128)(2,1)}, bf16[128,2048]{1,0:T(8,128)(2,1)}) custom-call(s32[16,32]{1,0:T(8,128)} %bitcast.1, s32[32]{0:T(128)} %prompt_hbm.1, s32[32,128]{1,0:T(8,128)S(1)} %get-tuple-element.7.bounds_ref, bf16[128,2048]{1,0:T(8,128)(2,1)S(1)} %get-tuple-element.8.layer_ref, ...), custom_call_target="tpu_custom_call" | custom-call | tf_op jit(solution)/shard_map/fill_pages/pallas_call | solution.py:82

commit v8 on v7

--- a/solution.py
+++ b/solution.py
@@ -632,10 +632,12 @@
             pump_b(4 * j + 1)
 
     act = ownbuf[...]
+    for n in range(SUBS):
+        send2f[n] = down_part(act, n)
     pump_b(14)
     pump_b(15)
     for n in range(SUBS):
-        part = add_arrived(down_part(act, n), *ring2, SIDE - 2, n)
+        part = add_arrived(send2f[n], *ring2, SIDE - 2, n)
         for d in range(2):
             before = abuf[x, d, :, :, n * piece : (n + 1) * piece].reshape(HALF, piece).astype(jnp.float32)
             total = before + part[d * HALF : (d + 1) * HALF]

time: 91.8 us -> 91.5 us (level)
  no operation moved by 1% of the time
where the time goes in v8:
time: 91.5 us; the launch traced here: 91.2 us
  Pallas kernels  90.6 us (99%)
    pallas_call x1, Pallas kernels, run_layer(): pl.pallas_call(layer_kernel, out_shape=(pltpu.VMEM((rows, width), bf16),...  85.4 us
    pallas_call x1, Pallas kernels, fill_pages(): pl.pallas_call(fill_kernel, out_shape=(jax.ShapeDtypeStruct((requests * m...  5.17 us

profile of v8, /device:TPU:0, one launch (start us, length us, event | category | flops | bytes accessed | tf_op | source)
XLA Modules:
  0.0 91.2 jit_solution(7012818417535846003)
XLA Ops:
  0.6 85.4 %layer.1 = (bf16[128,2048]{1,0:T(8,128)(2,1)S(1)}, bf16[16384,2,256]{2,1,0:T(2,128)(2,1)S(1)}, s32[32,128]{1,0:T(8,128)S(1)}) custom-call(bf16[128,2048]{1,0:T(8,128)(2,1)} %hidden.1, s32[32,512]{1,0:T(8,128)} %seg_hbm.1, bf16[2048]{0:T(1024)(128)(2,1)} %ln_attn_hbm.1, bf16[2048,512]{1,0:T(8,128)(2,1)} %w_query.1, bf16[2048,256]{1,0:T(8,128)(2,1)} %w_key.1, ...), custom_call_target="tpu_custom_call" | custom-call | tf_op jit(solution)/shard_map/layer/pallas_call | solution.py:685
  86.0 5.2 %fill_pages.1 = (bf16[512,16,2,256]{3,2,1,0:T(2,128)(2,1)}, bf16[128,2048]{1,0:T(8,128)(2,1)}) custom-call(s32[16,32]{1,0:T(8,128)} %bitcast.1, s32[32]{0:T(128)} %prompt_hbm.1, s32[32,128]{1,0:T(8,128)S(1)} %get-tuple-element.7.bounds_ref, bf16[128,2048]{1,0:T(8,128)(2,1)S(1)} %get-tuple-element.8.layer_ref, ...), custom_call_target="tpu_custom_call" | custom-call | tf_op jit(solution)/shard_map/fill_pages/pallas_call | solution.py:82
